TPU v7x, 512 devices: a whole 4x4x16 slice. The times are simulated.
512 devices in a mesh: branch: 8 (over z_lo), dp: 64 (over x, y, z_hi, core).
Axes of the slice: x: 4, y: 4, z: 16 (z_hi: 2, z_lo: 8; z = z_hi * 8 + z_lo), core: 2. Of those that a mesh axis runs over, the one named last changes fastest.
Arguments:
- tokens: bfloat16 [512, 4096], P('dp'), may hold values from -6 to 6
- routes: int32 [512, 2], P('dp'), may hold values from 0 to 7, all different within a row; in each aligned block of 8 rows (0 to 7, 8 to 15, ...) at most 4 rows name the same one
- route_weights: float32 [512, 2], P('dp'), may hold values from 0.2 to 1
- norm_gains: float32 [8, 4096], P('branch'), may hold values from 0.25 to 1.75
- keyval_weights: bfloat16 [8, 4096, 2048], P('branch', 'dp'), may hold values from -0.09375 to 0.09375
- expert_gate: bfloat16 [8, 4096, 8192], P('branch', None, 'dp'), may hold values from -0.09375 to 0.09375
- expert_up: bfloat16 [8, 4096, 8192], P('branch', None, 'dp'), may hold values from -0.09375 to 0.09375
- expert_down: bfloat16 [8, 8192, 4096], P('branch', None, 'dp'), may hold values from -0.0625 to 0.0625
Outputs:
- mixed: bfloat16 [512, 4096], P('dp')
- merged_keyval: bfloat16 [4096, 2048], P('dp', 'branch')
Inputs may be any that keep to these rules, and one draw needn't show every extreme that they name: `routes`: each token names 2 different experts. Among the 8 tokens of one dp index at most 4 name one expert, a bound that some block reaches.
All inputs are finite; a program needn't handle non-finite values.
Results may differ from a plain program's by a relative error of at most 0.013.
Values may be sent and summed in bfloat16 or wider, within the bound.
No kernel may reach another device: no remote copies, remote signals or barrier semaphores. Data moves between devices by JAX's collectives and lax.ppermute only.
A program may use at most 64 MiB of HBM per device.

v0:
```python
import jax
import jax.numpy as jnp
from jax import lax
from jax.sharding import PartitionSpec as P


def merge_keyval(keyval_weights, branches):
    summed = lax.psum_scatter(
        keyval_weights[0].astype(jnp.float32).astype(jnp.bfloat16),
        "branch",
        scatter_dimension=1,
        tiled=True,
    ).astype(jnp.float32)
    return (summed / branches).astype(jnp.bfloat16)


def normalize(block_rows, gain_avg):
    widened = block_rows.astype(jnp.float32)
    inv_rms = lax.rsqrt(jnp.mean(widened * widened, axis=1, keepdims=True) + 1e-05)
    return (widened * inv_rms * gain_avg[None, :]).astype(jnp.bfloat16)


def local(
    tokens, routes, route_weights, norm_gains, keyval_weights, expert_gate, expert_up, expert_down
):
    branches = lax.axis_size("branch")
    expert = lax.axis_index("branch")
    tok_count = tokens.shape[0]
    capacity = min(tok_count, 4 * tok_count // branches)
    merged_keyval = merge_keyval(keyval_weights, branches)
    gain_avg = lax.psum(norm_gains[0], "branch") / branches
    matched = routes == expert
    chosen = jnp.any(matched, axis=1)
    weight_share = jnp.sum(jnp.where(matched, route_weights, jnp.zeros_like(route_weights)), axis=1)
    slot_index = jnp.cumsum(chosen.astype(jnp.int32)) - 1
    picks = (
        (slot_index[None, :] == jnp.arange(capacity, dtype=jnp.int32)[:, None]) & chosen[None, :]
    ).astype(jnp.bfloat16)
    source_rows = normalize(tokens, gain_avg)
    packed = jnp.dot(picks, source_rows, preferred_element_type=jnp.float32).astype(jnp.bfloat16)
    block_rows = lax.all_gather(packed, "dp", axis=0, tiled=True)
    gate_part = jnp.dot(block_rows, expert_gate[0], preferred_element_type=jnp.float32)
    up_part = jnp.dot(block_rows, expert_up[0], preferred_element_type=jnp.float32)
    hidden = (jax.nn.silu(gate_part) * up_part).astype(jnp.bfloat16)
    down_rows = expert_down[0]
    result_cols = lax.dot_general(
        down_rows,
        lax.all_gather(hidden, "dp", axis=1, tiled=True),
        (((0,), (1,)), ((), ())),
        preferred_element_type=jnp.float32,
    ).astype(jnp.bfloat16)
    own_slots = lax.all_to_all(result_cols, "dp", split_axis=1, concat_axis=0, tiled=True)
    returned = (
        lax.dot_general(
            picks, own_slots, (((0,), (1,)), ((), ())), preferred_element_type=jnp.float32
        )
        * weight_share[:, None]
    )
    expert_total = lax.psum(returned, "branch")
    mixed = (tokens.astype(jnp.float32) + expert_total).astype(jnp.bfloat16)
    return (mixed, merged_keyval)


def solution(mesh):
    in_specs = (
        P("dp", None),
        P("dp", None),
        P("dp", None),
        P("branch", None),
        P("branch", "dp", None),
        P("branch", None, "dp"),
        P("branch", None, "dp"),
        P("branch", None, "dp"),
    )
    out_specs = (P("dp", None), P("dp", "branch"))
    return jax.shard_map(local, mesh=mesh, in_specs=in_specs, out_specs=out_specs, check_vma=False)
```

profile of v0, /device:TPU:6, one launch (start us, length us, event | category | flops | bytes accessed | tf_op | source)
XLA Modules:
  0.0 531.0 jit_solution(3716925837076763852)
XLA Ops:
  8.1 0.8 fusion.21
  8.8 0.2 reduce-window.8
  9.0 59.9 %psum.14 = f32[4096]{0:T(1024)S(1)} all-reduce(f32[4096]{0:T(1024)} %bitcast.33), channel_id=1, replica_groups=mesh['branch'=8,'dp'=64] {'branch'}, use_global_device_ids=true, to_apply=%region_3.4 | all-reduce | flops 4096 | bytes 32768 | tf_op jit(solution)/shard_map/psum | solution.py:31
  68.9 1.0 fusion.7
  69.9 1.7 fusion
  71.7 108.0 %all-gather.6.cloned.1.call-done = bf16[64,4,4096]{2,1,0:T(4,128)(2,1)} async-done(((bf16[1,4,4096]{2,1,0:T(4,128)(2,1)}), bf16[64,4,4096]{2,1,0:T(4,128)(2,1)}) %all-gather.6.cloned.1.call-update) | async-done | bytes 2097168 | tf_op jit(solution)/shard_map/all_gather | solution.py:41
  179.6 2.5 reshape.52
  182.2 0.7 fusion.5
  182.9 0.5 copy-done.4
  183.4 1.3 fusion.1
  184.8 134.9 %all-gather.4.cloned.1.call-done = bf16[256,8192]{1,0:T(8,128)(2,1)} async-done(((bf16[256,128]{1,0:T(8,128)(2,1)}), bf16[256,8192]{1,0:T(8,128)(2,1)}) %all-gather.4.cloned.1.call-update) | async-done | bytes 4194320 | tf_op jit(solution)/shard_map/all_gather | solution.py:48
  319.7 3.9 fusion.2
  323.6 0.1 copy.12
  323.7 0.7 reshape.53
  324.4 7.8 %all-to-all-start = ((bf16[64,2,128]{2,1,0:T(2,128)(2,1)}), bf16[64,2,128]{2,1,0:T(2,128)(2,1)S(1)}, u32[]{:S(2)}, u32[]{:S(2)}) async-start(bf16[64,2,128]{2,1,0:T(2,128)(2,1)} %reshape.53), calls=%async_computation | async-start | bytes 65536 | tf_op jit(solution)/shard_map/all_to_all | solution.py:52
  332.2 0.5 reduce-scatter.2.cloned.1.call-update
  332.9 14.1 %all-to-all-done = bf16[64,2,128]{2,1,0:T(2,128)(2,1)S(1)} async-done(((bf16[64,2,128]{2,1,0:T(2,128)(2,1)}), bf16[64,2,128]{2,1,0:T(2,128)(2,1)S(1)}, u32[]{:S(2)}, u32[]{:S(2)}) %all-to-all-start) | async-done | bytes 32800 | tf_op jit(solution)/shard_map/all_to_all | solution.py:52
  346.9 0.1 reshape.54
  347.1 0.1 all_to_all.17
  347.2 0.9 convolution_multiply_fusion
  348.1 55.8 %reduce-scatter.2.cloned.1.call-done = bf16[64,256]{1,0:T(8,128)(2,1)} async-done(((bf16[64,2048]{1,0:T(8,128)(2,1)}), bf16[64,256]{1,0:T(8,128)(2,1)}) %reduce-scatter.2.cloned.1.call-update) | async-done | bytes 32784 | tf_op jit(solution)/shard_map/reduce_scatter | solution.py:8
  403.9 1.4 multiply_convert_fusion
  405.3 116.7 %all-reduce.2.cloned.1.call-done = f32[8,4096]{1,0:T(8,128)} async-done(((f32[8,4096]{1,0:T(8,128)}), f32[8,4096]{1,0:T(8,128)}) %all-reduce.2.cloned.1.call-update) | async-done | bytes 131088 | tf_op jit(solution)/shard_map/psum | solution.py:59
  522.0 1.5 fusion.10
  (23 shorter events, 0.3 us)
Async XLA Ops:
  8.0 174.2 %copy-start = (bf16[1,4096,128]{2,1,0:T(8,128)(2,1)S(1)}, bf16[1,4096,128]{2,1,0:T(8,128)(2,1)}, u32[]{:S(2)}) copy-start(bf16[1,4096,128]{2,1,0:T(8,128)(2,1)} %param.13) | copy-start | bytes 3145732
  8.0 171.6 %all-gather.6.cloned.1.call-start = ((), (), s32[]{:S(2)}) async-start(), calls=%async_computation.5 | async-start | bytes 2129920 | tf_op jit(solution)/shard_map/all_gather | solution.py:41
  71.6 248.1 %all-gather.4.cloned.1.call-start = ((), (), s32[]{:S(2)}) async-start(), calls=%async_computation.2 | async-start | bytes 4259840 | tf_op jit(solution)/shard_map/all_gather | solution.py:48
  182.2 1.2 copy-start.4
  184.8 148.1 %copy-start.2 = (s32[8,2]{0,1:T(2,128)S(1)}, s32[8,2]{0,1:T(2,128)}, u32[]{:S(2)}) copy-start(s32[8,2]{0,1:T(2,128)} %param.9) | copy-start | bytes 196
  184.8 148.1 %copy-start.3 = (f32[8,2]{0,1:T(2,128)S(1)}, f32[8,2]{0,1:T(2,128)}, u32[]{:S(2)}) copy-start(f32[8,2]{0,1:T(2,128)} %param.10) | copy-start | bytes 196
  184.8 337.2 %copy-start.1 = (bf16[8,4096]{1,0:T(8,128)(2,1)S(1)}, bf16[8,4096]{1,0:T(8,128)(2,1)}, u32[]{:S(2)}) copy-start(bf16[8,4096]{1,0:T(8,128)(2,1)} %param.8) | copy-start | bytes 196612
  324.4 22.5 %all-to-all-start = ((bf16[64,2,128]{2,1,0:T(2,128)(2,1)}), bf16[64,2,128]{2,1,0:T(2,128)(2,1)S(1)}, u32[]{:S(2)}, u32[]{:S(2)}) async-start(bf16[64,2,128]{2,1,0:T(2,128)(2,1)} %reshape.53), calls=%async_computation | async-start | bytes 65536 | tf_op jit(solution)/shard_map/all_to_all | solution.py:52
  332.2 71.7 %reduce-scatter.2.cloned.1.call-start = ((), (), s32[]{:S(2)}) async-start(), calls=%async_computation.4 | async-start | bytes 294912 | tf_op jit(solution)/shard_map/reduce_scatter | solution.py:8
  332.8 189.2 %all-reduce.2.cloned.1.call-start = ((), (), s32[]{:S(2)}) async-start(), calls=%async_computation.3 | async-start | bytes 262144 | tf_op jit(solution)/shard_map/psum | solution.py:59
Sparse Core Ops, SparseCore 0:
  71.7 107.8 all-gather.5
  184.9 134.7 all-gather.3
Sparse Core Ops, SparseCore 1:
  335.5 68.4 reduce-scatter.1
  406.7 115.3 all-reduce.1
where the time goes:
time: 532 us; the launch traced here: 531 us
  waiting for transfers between devices  430 us (81%)
  blocking collectives  59.9 us (11%)
  between operations  15.6 us (3%)
  matrix products  8.44 us (2%)
  starting transfers between devices  7.95 us (1%)
    all_gather x1, waiting for transfers between devices, local(): lax.all_gather(hidden, 'dp', axis=1, tiled=True)  135 us
    psum x1, waiting for transfers between devices, local(): expert_total = lax.psum(returned, 'branch')  117 us
    all_gather x1, waiting for transfers between devices, local(): block_rows = lax.all_gather(packed, 'dp', axis=0, tiled=True)  108 us
    psum x1, blocking collectives, local(): gain_avg = lax.psum(norm_gains[0], 'branch') / branches  59.9 us
    reduce_scatter x1, waiting for transfers between devices, merge_keyval(): lax.psum_scatter(keyval_weights[0].astype(jnp.float32).astype(jnp.bfloat1...  55.8 us
    all_to_all x1, waiting for transfers between devices, local(): lax.all_to_all(result_cols, 'dp', split_axis=1, concat_axis=0, tiled=True)  14.1 us
  transfers between devices with their start and end apart: 5, of which 5 were waited for; matrix products, arithmetic and copies ran while one was open for 0% of the time, Pallas kernels for 0%

commit v1 on v0

v1 whole, which is shorter than its diff:
```python
import jax
import jax.numpy as jnp
from jax import lax
from jax.sharding import Mesh, PartitionSpec as P

F32 = jnp.float32
BF16 = jnp.bfloat16
XY = ("x", "y")
ZLINE = ("branch", "zh")
DP = ("x", "y", "zh", "core")
FLIP = [(0, 1), (1, 0)]


def route_tables(routes, route_weights, experts):
    matched = routes[:, :, None] == experts[None, None, :]
    chosen = jnp.any(matched, axis=1)
    share = jnp.sum(jnp.where(matched, route_weights[:, :, None], 0.0), axis=1)
    slot = jnp.cumsum(chosen.astype(jnp.int32), axis=0) - 1
    return chosen, share, slot


def local(
    tokens, routes, route_weights, norm_gains, keyval_weights, expert_gate, expert_up, expert_down
):
    experts = lax.axis_size("branch")
    n_xy = lax.axis_size("x") * lax.axis_size("y")
    expert = lax.axis_index("branch")
    half = lax.axis_index("zh")
    core = lax.axis_index("core")
    tok_count, width = tokens.shape
    cap = min(tok_count, 4 * tok_count // experts)
    group = 2 * cap

    wanted = jnp.stack([expert, (expert + experts // 2) % experts])
    chosen, _, slot = route_tables(routes, route_weights, wanted)
    rows = jnp.arange(group, dtype=jnp.int32)
    picks = (
        chosen.T[:, None, :]
        & (slot.T[:, None, :] == (rows % cap)[None, :, None])
        & (rows // cap == half)[None, :, None]
    ).astype(BF16)
    packed = jnp.dot(
        picks.reshape(2 * group, tok_count), tokens, preferred_element_type=F32
    ).astype(BF16)
    swap = [
        (2 * e + z, 2 * ((e + experts // 2) % experts) + 1 - z)
        for e in range(experts)
        for z in range(2)
    ]
    arrived = lax.ppermute(packed[group:], ZLINE, swap)
    both = packed[:group] + arrived
    spread = jnp.broadcast_to(both[None], (n_xy, group, width))
    mine = lax.all_to_all(spread, XY, 0, 0, tiled=True).reshape(n_xy * group, width)
    theirs = lax.ppermute(mine, "core", FLIP)

    kv = keyval_weights[0]
    kv_cols = kv.shape[1] // experts
    gain = norm_gains[0]
    gain_hi = lax.reduce_precision(gain, 8, 7)
    gain_lo = lax.reduce_precision(gain - gain_hi, 8, 7)
    gain_rows = jnp.stack([gain_hi, gain_lo]).astype(BF16).reshape(-1, kv_cols)
    kv_parts = kv.reshape(kv.shape[0], experts, kv_cols).swapaxes(0, 1)
    side = jnp.concatenate(
        [kv_parts, jnp.broadcast_to(gain_rows[None], (experts,) + gain_rows.shape)], axis=1
    )
    side = lax.all_to_all(side, "branch", 0, 0, tiled=True)
    side_sum = jnp.sum(side.astype(F32), axis=0) / experts
    merged_keyval = side_sum[: kv.shape[0]].astype(BF16)
    gain_avg = jnp.sum(side_sum[kv.shape[0] :].reshape(2, width), axis=0)

    def hidden_of(block):
        widened = block.astype(F32)
        inv_rms = lax.rsqrt(jnp.mean(widened * widened, axis=1, keepdims=True) + 1e-05)
        normed = (widened * inv_rms * gain_avg[None, :]).astype(BF16)
        gate = jnp.dot(normed, expert_gate[0], preferred_element_type=F32)
        up = jnp.dot(normed, expert_up[0], preferred_element_type=F32)
        return (jax.nn.silu(gate) * up).astype(BF16)

    hid_mine, hid_theirs = hidden_of(mine), hidden_of(theirs)
    units = hid_mine.shape[1]
    hid = jnp.stack(
        [
            jnp.where(core == 0, hid_mine, hid_theirs).reshape(n_xy, group, units),
            jnp.where(core == 0, hid_theirs, hid_mine).reshape(n_xy, group, units),
        ],
        axis=1,
    ).reshape(2 * n_xy * group, units)
    hid_far = lax.ppermute(hid, "zh", FLIP)
    hid = jnp.concatenate(
        [jnp.where(half == 0, hid, hid_far), jnp.where(half == 0, hid_far, hid)], axis=1
    )
    hid = lax.all_gather(hid, "core", axis=0, tiled=False)
    hid = jnp.concatenate([hid[0], hid[1]], axis=1)

    down = expert_down[0].T
    cols = down.shape[0]
    down = down.reshape(cols, n_xy, 2, 2, units).transpose(1, 0, 3, 2, 4)
    down = down.reshape(n_xy, cols, 4 * units)
    down = lax.all_to_all(down, XY, 0, 0, tiled=True).reshape(n_xy * cols, 4 * units)
    part = lax.dot_general(
        hid, down, (((1,), (1,)), ((), ())), preferred_element_type=F32
    ).astype(BF16)
    part = part.reshape(n_xy, 2 * group, n_xy * cols)
    part = lax.all_to_all(part, XY, 0, 0, tiled=True)
    total = jnp.sum(part.astype(F32), axis=0).astype(BF16)
    keep = jnp.where(core == 0, total[:group], total[group:])
    give = jnp.where(core == 0, total[group:], total[:group])
    got = lax.ppermute(give, "core", FLIP)
    whole = jnp.stack(
        [
            jnp.where(core == 0, keep, got).reshape(2, cap, n_xy, cols),
            jnp.where(core == 0, got, keep).reshape(2, cap, n_xy, cols),
        ],
        axis=3,
    ).reshape(2, cap, n_xy * 2 * cols)
    spread = jnp.broadcast_to(whole[None], (experts,) + whole.shape)
    spread = spread.reshape((2 * experts,) + whole.shape[1:])
    slots = lax.all_to_all(spread, ZLINE, 0, 0, tiled=True)
    slots = slots.reshape((experts, 2) + whole.shape[1:])

    chosen, share, slot = route_tables(routes, route_weights, jnp.arange(experts))
    mix = jnp.where(
        chosen[:, :, None] & (slot[:, :, None] == jnp.arange(cap)), share[:, :, None], 0.0
    )
    moe = jnp.einsum(
        "tes,ezsc->tzc", mix, slots.astype(F32), precision=lax.Precision.HIGHEST
    )
    moe = moe.reshape(tok_count, 2, n_xy, 2 * cols).swapaxes(1, 2).reshape(tok_count, width)
    mixed = (tokens.astype(F32) + moe).astype(BF16)
    return mixed, merged_keyval


def solution(mesh):
    n_x = n_y = int(round((mesh.devices.shape[1] // 4) ** 0.5))
    fine = Mesh(
        mesh.devices.reshape(mesh.devices.shape[0], n_x, n_y, 2, 2),
        ("branch", "x", "y", "zh", "core"),
    )
    in_specs = (
        P(DP, None),
        P(DP, None),
        P(DP, None),
        P("branch", None),
        P("branch", DP, None),
        P("branch", None, DP),
        P("branch", None, DP),
        P("branch", None, DP),
    )
    out_specs = (P(DP, None), P(DP, "branch"))
    return jax.shard_map(local, mesh=fine, in_specs=in_specs, out_specs=out_specs, check_vma=False)
```

time: 532 us -> 159 us (0.30)
  the two profiles are of different devices: /device:TPU:6 before, /device:TPU:32 now
where the time goes in v1:
time: 159 us; the launch traced here: 158 us
  waiting for transfers between devices  59.4 us (37%)
  starting transfers between devices  54.8 us (34%)
  blocking collectives  20.8 us (13%)
  local copies, waits for them, and re-layouts  9.51 us (6%)
  matrix products  7.84 us (5%)
  other arithmetic  4.25 us (3%)
    all_to_all x1, waiting for transfers between devices, local(): slots = lax.all_to_all(spread, ZLINE, 0, 0, tiled=True)  20.4 us
    all_to_all x1, blocking collectives, local(): part = lax.all_to_all(part, XY, 0, 0, tiled=True)  18.8 us
    all_to_all x1, waiting for transfers between devices, local(): lax.all_to_all(spread, XY, 0, 0, tiled=True).reshape(n_xy * group, width)  15.3 us
    all_to_all x1, waiting for transfers between devices, local(): side = lax.all_to_all(side, 'branch', 0, 0, tiled=True)  11.9 us
    ppermute x1, starting transfers between devices, local(): arrived = lax.ppermute(packed[group:], ZLINE, swap)  11.8 us
    all_to_all x1, starting transfers between devices, local(): slots = lax.all_to_all(spread, ZLINE, 0, 0, tiled=True)  9.67 us
    ppermute x1, starting transfers between devices, local(): hid_far = lax.ppermute(hid, 'zh', FLIP)  9.37 us
    all_to_all x1, starting transfers between devices, local(): side = lax.all_to_all(side, 'branch', 0, 0, tiled=True)  8.9 us
  transfers between devices with their start and end apart: 8, of which 6 were waited for; matrix products, arithmetic and copies ran while one was open for 9% of the time, Pallas kernels for 0%

profile of v1, /device:TPU:32, one launch (start us, length us, event | category | flops | bytes accessed | tf_op | source)
XLA Modules:
  0.0 157.6 jit_solution(984342483211671718)
XLA Ops:
  3.1 11.8 %collective-permute-start = (bf16[8,4096]{1,0:T(8,128)(2,1)S(1)}, bf16[8,4096]{1,0:T(8,128)(2,1)S(1)}, u32[]{:S(2)}, u32[]{:S(2)}) collective-permute-start(bf16[8,4096]{1,0:T(8,128)(2,1)S(1)} %slice.38), channel_id=1, source_target_pairs={{0,258},{2,256},{64,322},{66,320},{128,386},{130,384},{192,450},{1... | collective-permute-start | bytes 196616 | tf_op jit(solution)/shard_map/ppermute | solution.py:50
  14.9 4.2 %collective-permute-done = bf16[8,4096]{1,0:T(8,128)(2,1)S(1)} collective-permute-done((bf16[8,4096]{1,0:T(8,128)(2,1)S(1)}, bf16[8,4096]{1,0:T(8,128)(2,1)S(1)}, u32[]{:S(2)}, u32[]{:S(2)}) %collective-permute-start) | collective-permute-done | bytes 65568 | tf_op jit(solution)/shard_map/ppermute | solution.py:50
  19.1 1.1 broadcast_in_dim.32
  20.2 7.2 %all-to-all-start = ((bf16[16,8,4096]{2,1,0:T(8,128)(2,1)}), bf16[16,8,4096]{2,1,0:T(8,128)(2,1)S(1)}, u32[]{:S(2)}, u32[]{:S(2)}) async-start(bf16[16,8,4096]{2,1,0:T(8,128)(2,1)} %broadcast_in_dim.32), calls=%async_computation | async-start | bytes 2097152 | tf_op jit(solution)/shard_map/all_to_all | solution.py:53
  28.5 15.3 %all-to-all-done = bf16[16,8,4096]{2,1,0:T(8,128)(2,1)S(1)} async-done(((bf16[16,8,4096]{2,1,0:T(8,128)(2,1)}), bf16[16,8,4096]{2,1,0:T(8,128)(2,1)S(1)}, u32[]{:S(2)}, u32[]{:S(2)}) %all-to-all-start) | async-done | bytes 1048608 | tf_op jit(solution)/shard_map/all_to_all | solution.py:53
  43.7 8.9 %all-to-all-start.1 = ((bf16[8,96,256]{2,1,0:T(8,128)(2,1)}), bf16[8,96,256]{2,1,0:T(8,128)(2,1)S(1)}, u32[]{:S(2)}, u32[]{:S(2)}) async-start(bf16[8,96,256]{2,1,0:T(8,128)(2,1)} %copy.64), calls=%async_computation.1 | async-start | bytes 786432 | tf_op jit(solution)/shard_map/all_to_all | solution.py:66
  52.6 1.5 reshape.132
  54.2 2.3 %copy.82 = bf16[64,16,2,2,128]{4,2,3,0,1:T(2,128)(2,1)S(1)} copy(bf16[64,16,2,2,128]{4,3,2,1,0:T(2,128)(2,1)} %reshape.132) | data formatting | bytes 2097152 | tf_op jit(solution)/shard_map/reshape | solution.py:97
  56.5 1.2 reshape.133
  57.7 1.9 %collective-permute-start.1 = (bf16[128,4096]{1,0:T(8,128)(2,1)S(1)}, bf16[128,4096]{1,0:T(8,128)(2,1)}, u32[]{:S(2)}, u32[]{:S(2)}) collective-permute-start(bf16[128,4096]{1,0:T(8,128)(2,1)S(1)} %bitcast.77), channel_id=1, source_target_pairs={{0,1},{1,0},{2,3},{3,2},{4,5},{5,4},{6,7},{7,6},{8,9},{9,8},{10,11... | collective-permute-start | bytes 3145736 | tf_op jit(solution)/shard_map/ppermute | solution.py:54
  59.9 11.9 %all-to-all-done.1 = bf16[8,96,256]{2,1,0:T(8,128)(2,1)S(1)} async-done(((bf16[8,96,256]{2,1,0:T(8,128)(2,1)}), bf16[8,96,256]{2,1,0:T(8,128)(2,1)S(1)}, u32[]{:S(2)}, u32[]{:S(2)}) %all-to-all-start.1) | async-done | bytes 393248 | tf_op jit(solution)/shard_map/all_to_all | solution.py:66
  71.8 4.1 %all-to-all-start.2 = ((bf16[16,64,512]{2,1,0:T(8,128)(2,1)}), bf16[16,64,512]{2,1,0:T(8,128)(2,1)S(1)}, u32[]{:S(2)}, u32[]{:S(2)}) async-start(bf16[16,64,512]{2,1,0:T(8,128)(2,1)} %reshape.133), calls=%async_computation.2 | async-start | bytes 2097152 | tf_op jit(solution)/shard_map/all_to_all | solution.py:99
  76.0 1.7 %fusion.13 = f32[128,128]{1,0:T(8,128)S(1)} fusion(bf16[1,4096,128]{2,1,0:T(8,128)(2,1)} %param.13, bf16[16,8,4096]{2,1,0:T(8,128)(2,1)S(1)} %all-to-all-done, f32[4096]{0:T(1024)S(1)} %reduce_sum.60, f32[16,8]{1,0:T(8,128)S(1)} %add_rsqrt_fusion), kind=kOutput, calls=%fused_computation.21 | convolution fusion | flops 136314880 | bytes 2179584 | tf_op jit(solution)/shard_map/dot_general | solution.py:75
  78.3 1.6 %fusion.3 = f32[128]{0:T(128)S(1)} fusion(bf16[128,4096]{1,0:T(8,128)(2,1)} %collective-permute-done.1), kind=kLoop, calls=%fused_computation.8 | loop fusion | flops 1572736 | bytes 1049088 | tf_op jit(solution)/shard_map/reduce_sum | solution.py:73
  79.9 1.7 %fusion.11 = f32[128,128]{1,0:T(8,128)S(1)} fusion(bf16[1,4096,128]{2,1,0:T(8,128)(2,1)S(1)} %copy-done.7, bf16[128,4096]{1,0:T(8,128)(2,1)} %collective-permute-done.1, f32[4096]{0:T(1024)S(1)} %reduce_sum.60, f32[128]{0:T(128)S(1)} %add_rsqrt_fusion.1), kind=kOutput, calls=%fused_computation.19 | convolution fusion | flops 136314880 | bytes 2179584 | tf_op jit(solution)/shard_map/dot_general | solution.py:75
  81.6 1.7 %select_bitcast_fusion.1 = (bf16[16,1,8,128]{3,2,1,0:T(8,128)(2,1)S(1)}, bf16[128,128]{1,0:T(8,128)(2,1)S(1)}) fusion(bf16[128,128]{1,0:T(8,128)(2,1)S(1)} %fusion.6, pred[]{:T(512)S(6)} %eq.91, f32[128,128]{1,0:T(8,128)S(1)} %fusion.11, bf16[1,4096,128]{2,1,0:T(8,128)(2,1)S(1)} %copy-done, bf16[128,4096]{1,0:T(8,128)(2,1)} %collective-permute-done.1, ...), kind=kOutput, calls=%fused_computation.41 | convolution fusion | flops 136429568 | bytes 2277889 | tf_op jit(solution)/shard_map/dot_general | solution.py:76
  83.4 9.4 %collective-permute-start.2 = (bf16[256,128]{1,0:T(8,128)(2,1)S(1)}, bf16[256,128]{1,0:T(8,128)(2,1)S(1)}, u32[]{:S(2)}, u32[]{:S(2)}) collective-permute-start(bf16[256,128]{1,0:T(8,128)(2,1)S(1)} %bitcast.84), channel_id=1, source_target_pairs={{0,2},{2,0},{1,3},{3,1},{4,6},{6,4},{5,7},{7,5},{8,10},{10,8},{9,1... | collective-permute-start | bytes 196616 | tf_op jit(solution)/shard_map/ppermute | solution.py:88
  92.8 6.5 %collective-permute-done.2 = bf16[256,128]{1,0:T(8,128)(2,1)S(1)} collective-permute-done((bf16[256,128]{1,0:T(8,128)(2,1)S(1)}, bf16[256,128]{1,0:T(8,128)(2,1)S(1)}, u32[]{:S(2)}, u32[]{:S(2)}) %collective-permute-start.2) | collective-permute-done | bytes 65568 | tf_op jit(solution)/shard_map/ppermute | solution.py:88
  99.4 2.0 %all-gather = bf16[512,256]{1,0:T(8,128)(2,1)S(1)} all-gather(bf16[256,256]{1,0:T(8,128)(2,1)S(1)} %pad_maximum_fusion.1), channel_id=2, replica_groups=mesh['branch'=8,'x'=4,'y'=4,'zh'=2,'core'=2] {'core'}, dimensions={0}, use_global_device_ids=true | all-gather | bytes 393216 | tf_op jit(solution)/shard_map/all_gather | solution.py:92
  101.9 18.8 %all_to_all.25 = bf16[16,16,1024]{2,1,0:T(8,128)(2,1)S(1)} all-to-all(bf16[16,16,1024]{2,1,0:T(8,128)(2,1)S(1)} %bitcast.79), channel_id=1, replica_groups=mesh['branch'=8,'x'=4,'y'=4,'zh'=2,'core'=2] {'x','y'}, dimensions={0} | all-to-all | bytes 1048576 | tf_op jit(solution)/shard_map/all_to_all | solution.py:104
  120.8 1.9 %collective-permute-start.3 = (bf16[8,1024]{1,0:T(8,128)(2,1)S(1)}, bf16[8,1024]{1,0:T(8,128)(2,1)S(1)}, u32[]{:S(2)}, u32[]{:S(2)}) collective-permute-start(bf16[8,1024]{1,0:T(8,128)(2,1)S(1)} %broadcast_select_fusion.4), channel_id=1, source_target_pairs={{0,1},{1,0},{2,3},{3,2},{4,5},{5,4},{6,7},{7,6},{8,9},{9,8},{10,11... | collective-permute-start | bytes 49160 | tf_op jit(solution)/shard_map/ppermute | solution.py:108
  122.7 1.1 collective-permute-done.3
  125.1 9.7 %all-to-all-start.4 = ((bf16[16,4,2048]{2,1,0:T(4,128)(2,1)}), bf16[16,4,2048]{2,1,0:T(4,128)(2,1)S(1)}, u32[]{:S(2)}, u32[]{:S(2)}) async-start(bf16[16,4,2048]{2,1,0:T(4,128)(2,1)} %bitcast.23), calls=%async_computation.4 | async-start | bytes 524288 | tf_op jit(solution)/shard_map/all_to_all | solution.py:118
  135.6 20.4 %all-to-all-done.4 = bf16[16,4,2048]{2,1,0:T(4,128)(2,1)S(1)} async-done(((bf16[16,4,2048]{2,1,0:T(4,128)(2,1)}), bf16[16,4,2048]{2,1,0:T(4,128)(2,1)S(1)}, u32[]{:S(2)}, u32[]{:S(2)}) %all-to-all-start.4) | async-done | bytes 262176 | tf_op jit(solution)/shard_map/all_to_all | solution.py:118
  (74 shorter events, 8.7 us)
Async XLA Ops:
  0.6 77.1 %copy-start = (bf16[1,4096,128]{2,1,0:T(8,128)(2,1)S(1)}, bf16[1,4096,128]{2,1,0:T(8,128)(2,1)}, u32[]{:S(2)}) copy-start(bf16[1,4096,128]{2,1,0:T(8,128)(2,1)} %param.14) | copy-start | bytes 3145732
  3.1 16.0 %collective-permute-start = (bf16[8,4096]{1,0:T(8,128)(2,1)S(1)}, bf16[8,4096]{1,0:T(8,128)(2,1)S(1)}, u32[]{:S(2)}, u32[]{:S(2)}) collective-permute-start(bf16[8,4096]{1,0:T(8,128)(2,1)S(1)} %slice.38), channel_id=1, source_target_pairs={{0,258},{2,256},{64,322},{66,320},{128,386},{130,384},{192,450},{1... | collective-permute-start | bytes 196616 | tf_op jit(solution)/shard_map/ppermute | solution.py:50
  20.2 7.2 %copy-start.4 = (f32[1,4096]{1,0:T(1,128)S(1)}, f32[1,4096]{1,0:T(1,128)}, u32[]{:S(2)}) copy-start(f32[1,4096]{1,0:T(1,128)} %param.11) | copy-start | bytes 49156
  20.2 7.3 %copy-start.2 = (bf16[1,64,2048]{2,1,0:T(8,128)(2,1)S(1)}, bf16[1,64,2048]{2,1,0:T(8,128)(2,1)}, u32[]{:S(2)}) copy-start(bf16[1,64,2048]{2,1,0:T(8,128)(2,1)} %param.12) | copy-start | bytes 786436
  20.2 23.6 %all-to-all-start = ((bf16[16,8,4096]{2,1,0:T(8,128)(2,1)}), bf16[16,8,4096]{2,1,0:T(8,128)(2,1)S(1)}, u32[]{:S(2)}, u32[]{:S(2)}) async-start(bf16[16,8,4096]{2,1,0:T(8,128)(2,1)} %broadcast_in_dim.32), calls=%async_computation | async-start | bytes 2097152 | tf_op jit(solution)/shard_map/all_to_all | solution.py:53
  27.6 25.1 %copy-start.1 = (bf16[1,8192,64]{1,2,0:T(8,128)(2,1)S(1)}, bf16[1,8192,64]{1,2,0:T(8,128)(2,1)}, u32[]{:S(2)}) copy-start(bf16[1,8192,64]{1,2,0:T(8,128)(2,1)} %param.15) | copy-start | bytes 3145732
  43.7 28.0 %all-to-all-start.1 = ((bf16[8,96,256]{2,1,0:T(8,128)(2,1)}), bf16[8,96,256]{2,1,0:T(8,128)(2,1)S(1)}, u32[]{:S(2)}, u32[]{:S(2)}) async-start(bf16[8,96,256]{2,1,0:T(8,128)(2,1)} %copy.64), calls=%async_computation.1 | async-start | bytes 786432 | tf_op jit(solution)/shard_map/all_to_all | solution.py:66
  57.7 20.6 %collective-permute-start.1 = (bf16[128,4096]{1,0:T(8,128)(2,1)S(1)}, bf16[128,4096]{1,0:T(8,128)(2,1)}, u32[]{:S(2)}, u32[]{:S(2)}) collective-permute-start(bf16[128,4096]{1,0:T(8,128)(2,1)S(1)} %bitcast.77), channel_id=1, source_target_pairs={{0,1},{1,0},{2,3},{3,2},{4,5},{5,4},{6,7},{7,6},{8,9},{9,8},{10,11... | collective-permute-start | bytes 3145736 | tf_op jit(solution)/shard_map/ppermute | solution.py:54
  71.8 29.6 %all-to-all-start.2 = ((bf16[16,64,512]{2,1,0:T(8,128)(2,1)}), bf16[16,64,512]{2,1,0:T(8,128)(2,1)S(1)}, u32[]{:S(2)}, u32[]{:S(2)}) async-start(bf16[16,64,512]{2,1,0:T(8,128)(2,1)} %reshape.133), calls=%async_computation.2 | async-start | bytes 2097152 | tf_op jit(solution)/shard_map/all_to_all | solution.py:99
  78.3 1.6 %copy-start.7 = (bf16[1,4096,128]{2,1,0:T(8,128)(2,1)S(1)}, bf16[1,4096,128]{2,1,0:T(8,128)(2,1)}, u32[]{:S(2)}) copy-start(bf16[1,4096,128]{2,1,0:T(8,128)(2,1)} %param.13) | copy-start | bytes 3145732
  83.4 15.9 %collective-permute-start.2 = (bf16[256,128]{1,0:T(8,128)(2,1)S(1)}, bf16[256,128]{1,0:T(8,128)(2,1)S(1)}, u32[]{:S(2)}, u32[]{:S(2)}) collective-permute-start(bf16[256,128]{1,0:T(8,128)(2,1)S(1)} %bitcast.84), channel_id=1, source_target_pairs={{0,2},{2,0},{1,3},{3,1},{4,6},{6,4},{5,7},{7,5},{8,10},{10,8},{9,1... | collective-permute-start | bytes 196616 | tf_op jit(solution)/shard_map/ppermute | solution.py:88
  120.7 14.1 %copy-start.5 = (s32[8,2]{0,1:T(2,128)S(1)}, s32[8,2]{0,1:T(2,128)}, u32[]{:S(2)}) copy-start(s32[8,2]{0,1:T(2,128)} %param.9) | copy-start | bytes 196
  120.7 14.2 %copy-start.6 = (f32[8,2]{0,1:T(2,128)S(1)}, f32[8,2]{0,1:T(2,128)}, u32[]{:S(2)}) copy-start(f32[8,2]{0,1:T(2,128)} %param.10) | copy-start | bytes 196
  120.8 3.1 %collective-permute-start.3 = (bf16[8,1024]{1,0:T(8,128)(2,1)S(1)}, bf16[8,1024]{1,0:T(8,128)(2,1)S(1)}, u32[]{:S(2)}, u32[]{:S(2)}) collective-permute-start(bf16[8,1024]{1,0:T(8,128)(2,1)S(1)} %broadcast_select_fusion.4), channel_id=1, source_target_pairs={{0,1},{1,0},{2,3},{3,2},{4,5},{5,4},{6,7},{7,6},{8,9},{9,8},{10,11... | collective-permute-start | bytes 49160 | tf_op jit(solution)/shard_map/ppermute | solution.py:108
  125.1 31.9 %copy-start.3 = (bf16[8,4096]{1,0:T(8,128)(2,1)S(1)}, bf16[8,4096]{1,0:T(8,128)(2,1)}, u32[]{:S(2)}) copy-start(bf16[8,4096]{1,0:T(8,128)(2,1)} %param.8) | copy-start | bytes 196612
  125.1 30.8 %all-to-all-start.4 = ((bf16[16,4,2048]{2,1,0:T(4,128)(2,1)}), bf16[16,4,2048]{2,1,0:T(4,128)(2,1)S(1)}, u32[]{:S(2)}, u32[]{:S(2)}) async-start(bf16[16,4,2048]{2,1,0:T(4,128)(2,1)} %bitcast.23), calls=%async_computation.4 | async-start | bytes 524288 | tf_op jit(solution)/shard_map/all_to_all | solution.py:118

commit v2 on v1

--- a/solution.py
+++ b/solution.py
@@ -1,6 +1,10 @@
+import functools
+
 import jax
 import jax.numpy as jnp
 from jax import lax
+from jax.experimental import pallas as pl
+from jax.experimental.pallas import tpu as pltpu
 from jax.sharding import Mesh, PartitionSpec as P
 
 F32 = jnp.float32
@@ -11,6 +15,25 @@
 FLIP = [(0, 1), (1, 0)]
 
 
+def split_kernel(parts, source, target):
+    span = source.shape[1] // parts
+    for part in range(parts):
+        target[part] = source[:, part * span : (part + 1) * span]
+
+
+def split_columns(array, parts):
+    rows, cols = array.shape
+    return pl.pallas_call(
+        functools.partial(split_kernel, parts),
+        out_shape=jax.ShapeDtypeStruct((parts, rows, cols // parts), array.dtype),
+        cost_estimate=pl.CostEstimate(
+            flops=0, bytes_accessed=4 * rows * cols, transcendentals=0
+        ),
+        compiler_params=pltpu.CompilerParams(vmem_limit_bytes=8 << 20),
+        name="split_columns",
+    )(array)
+
+
 def route_tables(routes, route_weights, experts):
     matched = routes[:, :, None] == experts[None, None, :]
     chosen = jnp.any(matched, axis=1)
@@ -19,7 +42,7 @@
     return chosen, share, slot
 
 
-def local(
+def layer(
     tokens, routes, route_weights, norm_gains, keyval_weights, expert_gate, expert_up, expert_down
 ):
     experts = lax.axis_size("branch")
@@ -53,20 +76,33 @@
     mine = lax.all_to_all(spread, XY, 0, 0, tiled=True).reshape(n_xy * group, width)
     theirs = lax.ppermute(mine, "core", FLIP)
 
-    kv = keyval_weights[0]
-    kv_cols = kv.shape[1] // experts
-    gain = norm_gains[0]
+    kv, gain, _ = lax.optimization_barrier((keyval_weights[0], norm_gains, packed))
+    kv_rows = kv.shape[0]
     gain_hi = lax.reduce_precision(gain, 8, 7)
     gain_lo = lax.reduce_precision(gain - gain_hi, 8, 7)
-    gain_rows = jnp.stack([gain_hi, gain_lo]).astype(BF16).reshape(-1, kv_cols)
-    kv_parts = kv.reshape(kv.shape[0], experts, kv_cols).swapaxes(0, 1)
-    side = jnp.concatenate(
-        [kv_parts, jnp.broadcast_to(gain_rows[None], (experts,) + gain_rows.shape)], axis=1
-    )
-    side = lax.all_to_all(side, "branch", 0, 0, tiled=True)
-    side_sum = jnp.sum(side.astype(F32), axis=0) / experts
-    merged_keyval = side_sum[: kv.shape[0]].astype(BF16)
-    gain_avg = jnp.sum(side_sum[kv.shape[0] :].reshape(2, width), axis=0)
+    gain_pair = jnp.concatenate([gain_hi, gain_lo], axis=0).astype(BF16)
+    acc = kv
+    gain_sum = None
+    step = experts // 2
+    while step:
+        span = acc.shape[1] // 2
+        upper = (expert // step) % 2 == 1
+        stay = jnp.where(upper, acc[:, span:], acc[:, :span])
+        leave = jnp.where(upper, acc[:, :span], acc[:, span:])
+        extra = (gain_pair if gain_sum is None else gain_sum).reshape(-1, span)
+        turn = [(e, e ^ step) for e in range(experts)]
+        came = lax.ppermute(jnp.concatenate([leave, extra], axis=0), "branch", turn)
+        came, _ = lax.optimization_barrier((came, spread))
+        came = came.astype(F32)
+        acc = stay.astype(F32) + came[:kv_rows]
+        other = came[kv_rows:].reshape(-1, width)
+        if gain_sum is None:
+            gain_sum = gain + jnp.sum(other, axis=0, keepdims=True)
+        else:
+            gain_sum = gain_sum + other
+        step //= 2
+    merged_keyval = (acc / experts).astype(BF16)
+    gain_avg = gain_sum[0] / experts
 
     def hidden_of(block):
         widened = block.astype(F32)
@@ -90,12 +126,13 @@
         [jnp.where(half == 0, hid, hid_far), jnp.where(half == 0, hid_far, hid)], axis=1
     )
     hid = lax.all_gather(hid, "core", axis=0, tiled=False)
-    hid = jnp.concatenate([hid[0], hid[1]], axis=1)
+    hid = jnp.concatenate(
+        [hid[0, :, :units], hid[1, :, :units], hid[0, :, units:], hid[1, :, units:]], axis=1
+    )
 
-    down = expert_down[0].T
+    down, _ = lax.optimization_barrier((expert_down[0].T, spread))
     cols = down.shape[0]
-    down = down.reshape(cols, n_xy, 2, 2, units).transpose(1, 0, 3, 2, 4)
-    down = down.reshape(n_xy, cols, 4 * units)
+    down = split_columns(down, n_xy)
     down = lax.all_to_all(down, XY, 0, 0, tiled=True).reshape(n_xy * cols, 4 * units)
     part = lax.dot_general(
         hid, down, (((1,), (1,)), ((), ())), preferred_element_type=F32
@@ -147,4 +184,4 @@
         P("branch", None, DP),
     )
     out_specs = (P(DP, None), P(DP, "branch"))
-    return jax.shard_map(local, mesh=fine, in_specs=in_specs, out_specs=out_specs, check_vma=False)
+    return jax.shard_map(layer, mesh=fine, in_specs=in_specs, out_specs=out_specs, check_vma=False)

time: 159 us -> 150 us (0.943)
  other arithmetic: 4.25 us -> 9.46 us
  waiting for transfers between devices: 59.4 us -> 54.2 us
  local copies, waits for them, and re-layouts: 9.51 us -> 4.34 us
  matrix products: 7.84 us -> 4.2 us
    all_to_all x4 -> x3, waiting for transfers between devices: 47.5 us -> 26.7 us  [the longest x1 20.3 us: layer(): slots = lax.all_to_all(spread, ZLINE, 0, 0, tiled=True)]
    ppermute x4 -> x7, waiting for transfers between devices: 11.9 us -> 27.5 us  [the longest x3 13.3 us: layer(): came = lax.ppermute(jnp.concatenate([leave, extra], axis=0), 'branch', turn)]
    all_to_all x4 -> x3, starting transfers between devices: 29.8 us -> 20.5 us  [the longest x1 9.76 us: layer(): slots = lax.all_to_all(spread, ZLINE, 0, 0, tiled=True)]
    ppermute x4 -> x7, starting transfers between devices: 25 us -> 33.6 us  [the longest x3 13.5 us: layer(): came = lax.ppermute(jnp.concatenate([leave, extra], axis=0), 'branch', turn)]
    reshape x5 -> x4, local copies, waits for them, and re-layouts: 5.18 us -> 0.14 us  [the longest x1 0.11 us: layer(): moe.reshape(tok_count, 2, n_xy, 2 * cols).swapaxes(1, 2)]
    add x1 -> x5, other arithmetic: 0.01 us -> 4.24 us  [the longest x1 1.99 us: layer(): gain_sum = gain_sum + other]
    dot_general x2, matrix products: 3.44 us -> 1.02 us  [hidden_of(): gate = jnp.dot(normed, expert_gate[0], preferred_element_type=F32)]
  transfers between devices with their start and end apart: 8 -> 10, of which waited for: 6 -> 7; matrix products, arithmetic and copies ran while one was open for 9% -> 6% of each run, Pallas kernels for 0% -> 1%
where the time goes in v2:
time: 150 us; the launch traced here: 149 us
  waiting for transfers between devices  54.2 us (36%)
  starting transfers between devices  54.1 us (36%)
  blocking collectives  20.7 us (14%)
  other arithmetic  9.46 us (6%)
  local copies, waits for them, and re-layouts  4.34 us (3%)
  matrix products  4.2 us (3%)
    all_to_all x1, waiting for transfers between devices, layer(): slots = lax.all_to_all(spread, ZLINE, 0, 0, tiled=True)  20.3 us
    all_to_all x1, blocking collectives, layer(): part = lax.all_to_all(part, XY, 0, 0, tiled=True)  18.7 us
    ppermute x3, starting transfers between devices, layer(): came = lax.ppermute(jnp.concatenate([leave, extra], axis=0), 'branch', turn)  13.5 us
    ppermute x3, waiting for transfers between devices, layer(): came = lax.ppermute(jnp.concatenate([leave, extra], axis=0), 'branch', turn)  13.3 us
    ppermute x1, starting transfers between devices, layer(): arrived = lax.ppermute(packed[group:], ZLINE, swap)  11.8 us
    ppermute x1, waiting for transfers between devices, layer(): hid_far = lax.ppermute(hid, 'zh', FLIP)  11.8 us
    all_to_all x1, starting transfers between devices, layer(): slots = lax.all_to_all(spread, ZLINE, 0, 0, tiled=True)  9.76 us
    all_to_all x1, starting transfers between devices, layer(): lax.all_to_all(spread, XY, 0, 0, tiled=True).reshape(n_xy * group, width)  7.05 us
  transfers between devices with their start and end apart: 10, of which 7 were waited for; matrix products, arithmetic and copies ran while one was open for 6% of the time, Pallas kernels for 1%

profile of v2, /device:TPU:32, one launch (start us, length us, event | category | flops | bytes accessed | tf_op | source)
XLA Modules:
  0.0 149.3 jit_solution(12011220483555755337)
XLA Ops:
  1.9 1.1 convolution_convert_fusion
  3.0 11.8 %collective-permute-start = (bf16[8,4096]{1,0:T(8,128)(2,1)S(1)}, bf16[8,4096]{1,0:T(8,128)(2,1)S(1)}, u32[]{:S(2)}, u32[]{:S(2)}) collective-permute-start(bf16[8,4096]{1,0:T(8,128)(2,1)S(1)} %slice.89), channel_id=1, source_target_pairs={{0,258},{2,256},{64,322},{66,320},{128,386},{130,384},{192,450},{1... | collective-permute-start | bytes 196616 | tf_op jit(solution)/shard_map/ppermute | solution.py:73
  16.7 5.6 %collective-permute-start.1 = (bf16[72,1024]{1,0:T(8,128)(2,1)S(1)}, bf16[72,1024]{1,0:T(8,128)(2,1)S(1)}, u32[]{:S(2)}, u32[]{:S(2)}) collective-permute-start(bf16[72,1024]{1,0:T(8,128)(2,1)S(1)} %pad_maximum_fusion), channel_id=1, source_target_pairs={{0,256},{64,320},{128,384},{192,448},{256,0},{320,64},{384,128},{4... | collective-permute-start | bytes 442376 | tf_op jit(solution)/shard_map/ppermute | solution.py:94
  22.4 12.0 %collective-permute-done.1 = bf16[72,1024]{1,0:T(8,128)(2,1)S(1)} collective-permute-done((bf16[72,1024]{1,0:T(8,128)(2,1)S(1)}, bf16[72,1024]{1,0:T(8,128)(2,1)S(1)}, u32[]{:S(2)}, u32[]{:S(2)}) %collective-permute-start.1) | collective-permute-done | bytes 147488 | tf_op jit(solution)/shard_map/ppermute | solution.py:94
  34.4 1.1 broadcast_in_dim.32
  36.1 1.3 fusion.50
  37.5 3.6 %collective-permute-start.2 = (f32[72,512]{1,0:T(8,128)S(1)}, f32[72,512]{1,0:T(8,128)}, u32[]{:S(2)}, u32[]{:S(2)}) collective-permute-start(f32[72,512]{1,0:T(8,128)S(1)} %pad_maximum_fusion.1), channel_id=1, source_target_pairs={{0,128},{64,192},{128,0},{192,64},{256,384},{320,448},{384,256},{4... | collective-permute-start | bytes 442376 | tf_op jit(solution)/shard_map/ppermute | solution.py:94
  41.1 7.0 %all-to-all-start = ((bf16[16,8,4096]{2,1,0:T(8,128)(2,1)}), bf16[16,8,4096]{2,1,0:T(8,128)(2,1)S(1)}, u32[]{:S(2)}, u32[]{:S(2)}) async-start(bf16[16,8,4096]{2,1,0:T(8,128)(2,1)} %broadcast_in_dim.32), calls=%async_computation | async-start | bytes 2097152 | tf_op jit(solution)/shard_map/all_to_all | solution.py:76
  49.0 2.0 %fusion.49 = (f32[4096]{0:T(1024)S(1)}, f32[1,4096]{1,0:T(1,128)}) fusion(f32[]{:T(128)} %broadcast.165, f32[1,4096]{1,0:T(1,128)} %get-tuple-element.19, f32[1,4096]{1,0:T(1,128)S(1)} %bitcast.99), kind=kLoop, calls=%fused_computation.99 | loop fusion | flops 4096 | bytes 65540 | tf_op jit(solution)/shard_map/add | solution.py:102
  52.0 4.3 %collective-permute-start.3 = (f32[80,256]{1,0:T(8,128)S(1)}, f32[80,256]{1,0:T(8,128)S(1)}, u32[]{:S(2)}, u32[]{:S(2)}) collective-permute-start(f32[80,256]{1,0:T(8,128)S(1)} %pad_maximum_fusion.3), channel_id=1, source_target_pairs={{0,64},{64,0},{128,192},{192,128},{256,320},{320,256},{384,448},{4... | collective-permute-start | bytes 245768 | tf_op jit(solution)/shard_map/ppermute | solution.py:94
  56.3 1.1 split_columns.1
  57.4 1.3 collective-permute-done.3
  58.7 6.4 %all-to-all-done = bf16[16,8,4096]{2,1,0:T(8,128)(2,1)S(1)} async-done(((bf16[16,8,4096]{2,1,0:T(8,128)(2,1)}), bf16[16,8,4096]{2,1,0:T(8,128)(2,1)S(1)}, u32[]{:S(2)}, u32[]{:S(2)}) %all-to-all-start) | async-done | bytes 1048608 | tf_op jit(solution)/shard_map/all_to_all | solution.py:76
  65.1 3.7 %all-to-all-start.1 = ((bf16[16,64,512]{2,1,0:T(8,128)(2,1)}), bf16[16,64,512]{2,1,0:T(8,128)(2,1)S(1)}, u32[]{:S(2)}, u32[]{:S(2)}) async-start(bf16[16,64,512]{2,1,0:T(8,128)(2,1)} %split_columns.1), calls=%async_computation.1 | async-start | bytes 2097152 | tf_op jit(solution)/shard_map/all_to_all | solution.py:136
  68.8 2.1 %collective-permute-start.4 = (bf16[128,4096]{1,0:T(8,128)(2,1)S(1)}, bf16[128,4096]{1,0:T(8,128)(2,1)S(1)}, u32[]{:S(2)}, u32[]{:S(2)}) collective-permute-start(bf16[128,4096]{1,0:T(8,128)(2,1)S(1)} %bitcast.89), channel_id=1, source_target_pairs={{0,1},{1,0},{2,3},{3,2},{4,5},{5,4},{6,7},{7,6},{8,9},{9,8},{10,11... | collective-permute-start | bytes 3145736 | tf_op jit(solution)/shard_map/ppermute | solution.py:77
  72.2 1.3 collective-permute-done.4
  74.8 4.3 %collective-permute-start.5 = (bf16[256,128]{1,0:T(8,128)(2,1)S(1)}, bf16[256,128]{1,0:T(8,128)(2,1)S(1)}, u32[]{:S(2)}, u32[]{:S(2)}) collective-permute-start(bf16[256,128]{1,0:T(8,128)(2,1)S(1)} %bitcast.96), channel_id=1, source_target_pairs={{0,2},{2,0},{1,3},{3,1},{4,6},{6,4},{5,7},{7,5},{8,10},{10,8},{9,1... | collective-permute-start | bytes 196616 | tf_op jit(solution)/shard_map/ppermute | solution.py:124
  79.2 11.8 %collective-permute-done.5 = bf16[256,128]{1,0:T(8,128)(2,1)S(1)} collective-permute-done((bf16[256,128]{1,0:T(8,128)(2,1)S(1)}, bf16[256,128]{1,0:T(8,128)(2,1)S(1)}, u32[]{:S(2)}, u32[]{:S(2)}) %collective-permute-start.5) | collective-permute-done | bytes 65568 | tf_op jit(solution)/shard_map/ppermute | solution.py:124
  91.0 2.0 %all-gather = bf16[512,256]{1,0:T(8,128)(2,1)S(1)} all-gather(bf16[256,256]{1,0:T(8,128)(2,1)S(1)} %pad_maximum_fusion.2), channel_id=2, replica_groups=mesh['branch'=8,'x'=4,'y'=4,'zh'=2,'core'=2] {'core'}, dimensions={0}, use_global_device_ids=true | all-gather | bytes 393216 | tf_op jit(solution)/shard_map/all_gather | solution.py:128
  93.5 18.7 %all_to_all.20 = bf16[16,16,1024]{2,1,0:T(8,128)(2,1)S(1)} all-to-all(bf16[16,16,1024]{2,1,0:T(8,128)(2,1)S(1)} %bitcast.95), channel_id=1, replica_groups=mesh['branch'=8,'x'=4,'y'=4,'zh'=2,'core'=2] {'x','y'}, dimensions={0} | all-to-all | bytes 1048576 | tf_op jit(solution)/shard_map/all_to_all | solution.py:141
  112.4 1.9 %collective-permute-start.6 = (bf16[8,1024]{1,0:T(8,128)(2,1)S(1)}, bf16[8,1024]{1,0:T(8,128)(2,1)S(1)}, u32[]{:S(2)}, u32[]{:S(2)}) collective-permute-start(bf16[8,1024]{1,0:T(8,128)(2,1)S(1)} %broadcast_select_fusion.5), channel_id=1, source_target_pairs={{0,1},{1,0},{2,3},{3,2},{4,5},{5,4},{6,7},{7,6},{8,9},{9,8},{10,11... | collective-permute-start | bytes 49160 | tf_op jit(solution)/shard_map/ppermute | solution.py:145
  114.3 1.1 collective-permute-done.6
  116.7 9.8 %all-to-all-start.3 = ((bf16[16,4,2048]{2,1,0:T(4,128)(2,1)}), bf16[16,4,2048]{2,1,0:T(4,128)(2,1)S(1)}, u32[]{:S(2)}, u32[]{:S(2)}) async-start(bf16[16,4,2048]{2,1,0:T(4,128)(2,1)} %bitcast.29), calls=%async_computation.3 | async-start | bytes 524288 | tf_op jit(solution)/shard_map/all_to_all | solution.py:155
  127.3 20.3 %all-to-all-done.3 = bf16[16,4,2048]{2,1,0:T(4,128)(2,1)S(1)} async-done(((bf16[16,4,2048]{2,1,0:T(4,128)(2,1)}), bf16[16,4,2048]{2,1,0:T(4,128)(2,1)S(1)}, u32[]{:S(2)}, u32[]{:S(2)}) %all-to-all-start.3) | async-done | bytes 262176 | tf_op jit(solution)/shard_map/all_to_all | solution.py:155
  (91 shorter events, 12.6 us)
Async XLA Ops:
  0.6 71.1 %copy-start = (bf16[1,4096,128]{2,1,0:T(8,128)(2,1)S(1)}, bf16[1,4096,128]{2,1,0:T(8,128)(2,1)}, u32[]{:S(2)}) copy-start(bf16[1,4096,128]{2,1,0:T(8,128)(2,1)} %param.14) | copy-start | bytes 3145732
  3.0 19.4 %collective-permute-start = (bf16[8,4096]{1,0:T(8,128)(2,1)S(1)}, bf16[8,4096]{1,0:T(8,128)(2,1)S(1)}, u32[]{:S(2)}, u32[]{:S(2)}) collective-permute-start(bf16[8,4096]{1,0:T(8,128)(2,1)S(1)} %slice.89), channel_id=1, source_target_pairs={{0,258},{2,256},{64,322},{66,320},{128,386},{130,384},{192,450},{1... | collective-permute-start | bytes 196616 | tf_op jit(solution)/shard_map/ppermute | solution.py:73
  16.7 19.4 %copy-start.4 = (f32[1,4096]{1,0:T(1,128)S(1)}, f32[1,4096]{1,0:T(1,128)}, u32[]{:S(2)}) copy-start(f32[1,4096]{1,0:T(1,128)} %param.11) | copy-start | bytes 49156
  16.7 20.7 %copy-start.2 = (bf16[1,64,2048]{2,1,0:T(8,128)(2,1)S(1)}, bf16[1,64,2048]{2,1,0:T(8,128)(2,1)}, u32[]{:S(2)}) copy-start(bf16[1,64,2048]{2,1,0:T(8,128)(2,1)} %param.12) | copy-start | bytes 786436
  16.7 17.7 %collective-permute-start.1 = (bf16[72,1024]{1,0:T(8,128)(2,1)S(1)}, bf16[72,1024]{1,0:T(8,128)(2,1)S(1)}, u32[]{:S(2)}, u32[]{:S(2)}) collective-permute-start(bf16[72,1024]{1,0:T(8,128)(2,1)S(1)} %pad_maximum_fusion), channel_id=1, source_target_pairs={{0,256},{64,320},{128,384},{192,448},{256,0},{320,64},{384,128},{4... | collective-permute-start | bytes 442376 | tf_op jit(solution)/shard_map/ppermute | solution.py:94
  37.5 10.7 %collective-permute-start.2 = (f32[72,512]{1,0:T(8,128)S(1)}, f32[72,512]{1,0:T(8,128)}, u32[]{:S(2)}, u32[]{:S(2)}) collective-permute-start(f32[72,512]{1,0:T(8,128)S(1)} %pad_maximum_fusion.1), channel_id=1, source_target_pairs={{0,128},{64,192},{128,0},{192,64},{256,384},{320,448},{384,256},{4... | collective-permute-start | bytes 442376 | tf_op jit(solution)/shard_map/ppermute | solution.py:94
  41.1 24.0 %all-to-all-start = ((bf16[16,8,4096]{2,1,0:T(8,128)(2,1)}), bf16[16,8,4096]{2,1,0:T(8,128)(2,1)S(1)}, u32[]{:S(2)}, u32[]{:S(2)}) async-start(bf16[16,8,4096]{2,1,0:T(8,128)(2,1)} %broadcast_in_dim.32), calls=%async_computation | async-start | bytes 2097152 | tf_op jit(solution)/shard_map/all_to_all | solution.py:76
  48.2 8.1 %copy-start.1 = (bf16[1,8192,64]{1,2,0:T(8,128)(2,1)S(1)}, bf16[1,8192,64]{1,2,0:T(8,128)(2,1)}, u32[]{:S(2)}) copy-start(bf16[1,8192,64]{1,2,0:T(8,128)(2,1)} %param.15) | copy-start | bytes 3145732
  52.0 6.7 %collective-permute-start.3 = (f32[80,256]{1,0:T(8,128)S(1)}, f32[80,256]{1,0:T(8,128)S(1)}, u32[]{:S(2)}, u32[]{:S(2)}) collective-permute-start(f32[80,256]{1,0:T(8,128)S(1)} %pad_maximum_fusion.3), channel_id=1, source_target_pairs={{0,64},{64,0},{128,192},{192,128},{256,320},{320,256},{384,448},{4... | collective-permute-start | bytes 245768 | tf_op jit(solution)/shard_map/ppermute | solution.py:94
  58.7 12.1 %copy-start.5 = (f32[1,4096]{1,0:T(1,128)S(1)}, f32[1,4096]{1,0:T(1,128)}, u32[]{:S(2)}) copy-start(f32[1,4096]{1,0:T(1,128)} %get-tuple-element.17) | copy-start | bytes 49156
  65.1 27.9 %all-to-all-start.1 = ((bf16[16,64,512]{2,1,0:T(8,128)(2,1)}), bf16[16,64,512]{2,1,0:T(8,128)(2,1)S(1)}, u32[]{:S(2)}, u32[]{:S(2)}) async-start(bf16[16,64,512]{2,1,0:T(8,128)(2,1)} %split_columns.1), calls=%async_computation.1 | async-start | bytes 2097152 | tf_op jit(solution)/shard_map/all_to_all | solution.py:136
  68.8 2.4 %copy-start.8 = (bf16[1,4096,128]{2,1,0:T(8,128)(2,1)S(1)}, bf16[1,4096,128]{2,1,0:T(8,128)(2,1)}, u32[]{:S(2)}) copy-start(bf16[1,4096,128]{2,1,0:T(8,128)(2,1)} %param.13) | copy-start | bytes 3145732
  68.8 4.7 %collective-permute-start.4 = (bf16[128,4096]{1,0:T(8,128)(2,1)S(1)}, bf16[128,4096]{1,0:T(8,128)(2,1)S(1)}, u32[]{:S(2)}, u32[]{:S(2)}) collective-permute-start(bf16[128,4096]{1,0:T(8,128)(2,1)S(1)} %bitcast.89), channel_id=1, source_target_pairs={{0,1},{1,0},{2,3},{3,2},{4,5},{5,4},{6,7},{7,6},{8,9},{9,8},{10,11... | collective-permute-start | bytes 3145736 | tf_op jit(solution)/shard_map/ppermute | solution.py:77
  74.8 16.1 %collective-permute-start.5 = (bf16[256,128]{1,0:T(8,128)(2,1)S(1)}, bf16[256,128]{1,0:T(8,128)(2,1)S(1)}, u32[]{:S(2)}, u32[]{:S(2)}) collective-permute-start(bf16[256,128]{1,0:T(8,128)(2,1)S(1)} %bitcast.96), channel_id=1, source_target_pairs={{0,2},{2,0},{1,3},{3,1},{4,6},{6,4},{5,7},{7,5},{8,10},{10,8},{9,1... | collective-permute-start | bytes 196616 | tf_op jit(solution)/shard_map/ppermute | solution.py:124
  112.3 14.2 %copy-start.6 = (s32[8,2]{0,1:T(2,128)S(1)}, s32[8,2]{0,1:T(2,128)}, u32[]{:S(2)}) copy-start(s32[8,2]{0,1:T(2,128)} %param.9) | copy-start | bytes 196
  112.3 14.3 %copy-start.7 = (f32[8,2]{0,1:T(2,128)S(1)}, f32[8,2]{0,1:T(2,128)}, u32[]{:S(2)}) copy-start(f32[8,2]{0,1:T(2,128)} %param.10) | copy-start | bytes 196
  112.4 3.1 %collective-permute-start.6 = (bf16[8,1024]{1,0:T(8,128)(2,1)S(1)}, bf16[8,1024]{1,0:T(8,128)(2,1)S(1)}, u32[]{:S(2)}, u32[]{:S(2)}) collective-permute-start(bf16[8,1024]{1,0:T(8,128)(2,1)S(1)} %broadcast_select_fusion.5), channel_id=1, source_target_pairs={{0,1},{1,0},{2,3},{3,2},{4,5},{5,4},{6,7},{7,6},{8,9},{9,8},{10,11... | collective-permute-start | bytes 49160 | tf_op jit(solution)/shard_map/ppermute | solution.py:145
  116.7 32.0 %copy-start.3 = (bf16[8,4096]{1,0:T(8,128)(2,1)S(1)}, bf16[8,4096]{1,0:T(8,128)(2,1)}, u32[]{:S(2)}) copy-start(bf16[8,4096]{1,0:T(8,128)(2,1)} %param.8) | copy-start | bytes 196612
  116.7 30.9 %all-to-all-start.3 = ((bf16[16,4,2048]{2,1,0:T(4,128)(2,1)}), bf16[16,4,2048]{2,1,0:T(4,128)(2,1)S(1)}, u32[]{:S(2)}, u32[]{:S(2)}) async-start(bf16[16,4,2048]{2,1,0:T(4,128)(2,1)} %bitcast.29), calls=%async_computation.3 | async-start | bytes 524288 | tf_op jit(solution)/shard_map/all_to_all | solution.py:155

commit v3 on v2

--- a/solution.py
+++ b/solution.py
@@ -53,6 +53,12 @@
     tok_count, width = tokens.shape
     cap = min(tok_count, 4 * tok_count // experts)
     group = 2 * cap
+    steps = [experts >> shift for shift in range(1, experts.bit_length())]
+
+    down = expert_down[0].T
+    cols = down.shape[0]
+    down = split_columns(down, n_xy)
+    down = lax.all_to_all(down, XY, 0, 0, tiled=True).reshape(n_xy * cols, -1)
 
     wanted = jnp.stack([expert, (expert + experts // 2) % experts])
     chosen, _, slot = route_tables(routes, route_weights, wanted)
@@ -73,35 +79,17 @@
     arrived = lax.ppermute(packed[group:], ZLINE, swap)
     both = packed[:group] + arrived
     spread = jnp.broadcast_to(both[None], (n_xy, group, width))
+    spread, down = lax.optimization_barrier((spread, down))
     mine = lax.all_to_all(spread, XY, 0, 0, tiled=True).reshape(n_xy * group, width)
     theirs = lax.ppermute(mine, "core", FLIP)
 
-    kv, gain, _ = lax.optimization_barrier((keyval_weights[0], norm_gains, packed))
-    kv_rows = kv.shape[0]
-    gain_hi = lax.reduce_precision(gain, 8, 7)
-    gain_lo = lax.reduce_precision(gain - gain_hi, 8, 7)
-    gain_pair = jnp.concatenate([gain_hi, gain_lo], axis=0).astype(BF16)
-    acc = kv
-    gain_sum = None
-    step = experts // 2
-    while step:
-        span = acc.shape[1] // 2
-        upper = (expert // step) % 2 == 1
-        stay = jnp.where(upper, acc[:, span:], acc[:, :span])
-        leave = jnp.where(upper, acc[:, :span], acc[:, span:])
-        extra = (gain_pair if gain_sum is None else gain_sum).reshape(-1, span)
+    gain_sum = norm_gains
+    for step in steps:
         turn = [(e, e ^ step) for e in range(experts)]
-        came = lax.ppermute(jnp.concatenate([leave, extra], axis=0), "branch", turn)
-        came, _ = lax.optimization_barrier((came, spread))
-        came = came.astype(F32)
-        acc = stay.astype(F32) + came[:kv_rows]
-        other = came[kv_rows:].reshape(-1, width)
-        if gain_sum is None:
-            gain_sum = gain + jnp.sum(other, axis=0, keepdims=True)
-        else:
-            gain_sum = gain_sum + other
-        step //= 2
-    merged_keyval = (acc / experts).astype(BF16)
+        came = lax.ppermute(gain_sum, "branch", turn)
+        if step == steps[0]:
+            came, _ = lax.optimization_barrier((came, spread))
+        gain_sum = gain_sum + came
     gain_avg = gain_sum[0] / experts
 
     def hidden_of(block):
@@ -130,14 +118,22 @@
         [hid[0, :, :units], hid[1, :, :units], hid[0, :, units:], hid[1, :, units:]], axis=1
     )
 
-    down, _ = lax.optimization_barrier((expert_down[0].T, spread))
-    cols = down.shape[0]
-    down = split_columns(down, n_xy)
-    down = lax.all_to_all(down, XY, 0, 0, tiled=True).reshape(n_xy * cols, 4 * units)
     part = lax.dot_general(
         hid, down, (((1,), (1,)), ((), ())), preferred_element_type=F32
     ).astype(BF16)
     part = part.reshape(n_xy, 2 * group, n_xy * cols)
+
+    acc, _ = lax.optimization_barrier((keyval_weights[0], hid_mine))
+    for step in steps:
+        span = acc.shape[1] // 2
+        upper = (expert // step) % 2 == 1
+        stay = jnp.where(upper, acc[:, span:], acc[:, :span])
+        leave = jnp.where(upper, acc[:, :span], acc[:, span:])
+        turn = [(e, e ^ step) for e in range(experts)]
+        came = lax.ppermute(leave, "branch", turn)
+        if step == steps[0]:
+            came, _ = lax.optimization_barrier((came, part))
+        acc = stay.astype(F32) + came.astype(F32)
     part = lax.all_to_all(part, XY, 0, 0, tiled=True)
     total = jnp.sum(part.astype(F32), axis=0).astype(BF16)
     keep = jnp.where(core == 0, total[:group], total[group:])
@@ -152,6 +148,8 @@
     ).reshape(2, cap, n_xy * 2 * cols)
     spread = jnp.broadcast_to(whole[None], (experts,) + whole.shape)
     spread = spread.reshape((2 * experts,) + whole.shape[1:])
+    acc, _ = lax.optimization_barrier((acc, spread))
+    merged_keyval = (acc / experts).astype(BF16)
     slots = lax.all_to_all(spread, ZLINE, 0, 0, tiled=True)
     slots = slots.reshape((experts, 2) + whole.shape[1:])
 

time: 150 us -> 150 us (level)
  the two profiles are of different devices: /device:TPU:32 before, /device:TPU:6 now
where the time goes in v3:
time: 150 us; the launch traced here: 149 us
  starting transfers between devices  87.6 us (58%)
  waiting for transfers between devices  46.2 us (31%)
  local copies, waits for them, and re-layouts  4.21 us (3%)
  matrix products  4.15 us (3%)
  other arithmetic  2.8 us (2%)
  blocking collectives  1.99 us (1%)
    ppermute x3, waiting for transfers between devices, layer(): came = lax.ppermute(leave, 'branch', turn)  21 us
    ppermute x3, starting transfers between devices, layer(): came = lax.ppermute(leave, 'branch', turn)  15 us
    ppermute x1, starting transfers between devices, layer(): hid_far = lax.ppermute(hid, 'zh', FLIP)  11.9 us
    ppermute x3, starting transfers between devices, layer(): came = lax.ppermute(gain_sum, 'branch', turn)  11.2 us
    ppermute x1, starting transfers between devices, layer(): arrived = lax.ppermute(packed[group:], ZLINE, swap)  10.8 us
    all_to_all x1, starting transfers between devices, layer(): slots = lax.all_to_all(spread, ZLINE, 0, 0, tiled=True)  10.5 us
    all_to_all x1, starting transfers between devices, layer(): down = lax.all_to_all(down, XY, 0, 0, tiled=True).reshape(n_xy * cols, -1)  9.47 us
    all_to_all x1, waiting for transfers between devices, layer(): slots = lax.all_to_all(spread, ZLINE, 0, 0, tiled=True)  8.75 us
  transfers between devices with their start and end apart: 14, of which 8 were waited for; matrix products, arithmetic and copies ran while one was open for 3% of the time, Pallas kernels for 0%

profile of v3, /device:TPU:6, one launch (start us, length us, event | category | flops | bytes accessed | tf_op | source)
XLA Modules:
  0.0 149.0 jit_solution(5004209086762639302)
XLA Ops:
  0.7 1.3 copy-done.1
  3.0 9.5 %all-to-all-start = ((bf16[16,64,512]{2,1,0:T(8,128)(2,1)}), bf16[16,64,512]{2,1,0:T(8,128)(2,1)S(1)}, u32[]{:S(2)}, u32[]{:S(2)}) async-start(bf16[16,64,512]{2,1,0:T(8,128)(2,1)} %split_columns.1), calls=%async_computation | async-start | bytes 2097152 | tf_op jit(solution)/shard_map/all_to_all | solution.py:61
  13.3 10.8 %collective-permute-start = (bf16[8,4096]{1,0:T(8,128)(2,1)S(1)}, bf16[8,4096]{1,0:T(8,128)(2,1)S(1)}, u32[]{:S(2)}, u32[]{:S(2)}) collective-permute-start(bf16[8,4096]{1,0:T(8,128)(2,1)S(1)} %slice.65), channel_id=1, source_target_pairs={{0,258},{2,256},{64,322},{66,320},{128,386},{130,384},{192,450},{1... | collective-permute-start | bytes 196616 | tf_op jit(solution)/shard_map/ppermute | solution.py:79
  24.1 5.0 %collective-permute-done = bf16[8,4096]{1,0:T(8,128)(2,1)S(1)} collective-permute-done((bf16[8,4096]{1,0:T(8,128)(2,1)S(1)}, bf16[8,4096]{1,0:T(8,128)(2,1)S(1)}, u32[]{:S(2)}, u32[]{:S(2)}) %collective-permute-start) | collective-permute-done | bytes 65568 | tf_op jit(solution)/shard_map/ppermute | solution.py:79
  30.2 7.4 %all-to-all-start.1 = ((bf16[16,8,4096]{2,1,0:T(8,128)(2,1)}), bf16[16,8,4096]{2,1,0:T(8,128)(2,1)S(1)}, u32[]{:S(2)}, u32[]{:S(2)}) async-start(bf16[16,8,4096]{2,1,0:T(8,128)(2,1)} %broadcast_in_dim.30), calls=%async_computation.1 | async-start | bytes 2097152 | tf_op jit(solution)/shard_map/all_to_all | solution.py:83
  37.6 6.2 %collective-permute-start.1 = (f32[1,4096]{1,0:T(1,128)S(1)}, f32[1,4096]{1,0:T(1,128)S(1)}, u32[]{:S(2)}, u32[]{:S(2)}) collective-permute-start(f32[1,4096]{1,0:T(1,128)S(1)} %copy-done.4), channel_id=1, source_target_pairs={{0,256},{64,320},{128,384},{192,448},{256,0},{320,64},{384,128},{4... | collective-permute-start | bytes 49160 | tf_op jit(solution)/shard_map/ppermute | solution.py:89
  43.8 3.4 %collective-permute-done.1 = f32[1,4096]{1,0:T(1,128)S(1)} collective-permute-done((f32[1,4096]{1,0:T(1,128)S(1)}, f32[1,4096]{1,0:T(1,128)S(1)}, u32[]{:S(2)}, u32[]{:S(2)}) %collective-permute-start.1) | collective-permute-done | bytes 16416 | tf_op jit(solution)/shard_map/ppermute | solution.py:89
  47.2 2.8 %collective-permute-start.2 = (f32[1,4096]{1,0:T(1,128)S(1)}, f32[1,4096]{1,0:T(1,128)S(1)}, u32[]{:S(2)}, u32[]{:S(2)}) collective-permute-start(f32[1,4096]{1,0:T(1,128)S(1)} %add.94), channel_id=1, source_target_pairs={{0,128},{64,192},{128,0},{192,64},{256,384},{320,448},{384,256},{4... | collective-permute-start | bytes 49160 | tf_op jit(solution)/shard_map/ppermute | solution.py:89
  50.0 3.7 %collective-permute-done.2 = f32[1,4096]{1,0:T(1,128)S(1)} collective-permute-done((f32[1,4096]{1,0:T(1,128)S(1)}, f32[1,4096]{1,0:T(1,128)S(1)}, u32[]{:S(2)}, u32[]{:S(2)}) %collective-permute-start.2) | collective-permute-done | bytes 16416 | tf_op jit(solution)/shard_map/ppermute | solution.py:89
  53.7 2.2 %collective-permute-start.3 = (f32[1,4096]{1,0:T(1,128)S(1)}, f32[1,4096]{1,0:T(1,128)S(1)}, u32[]{:S(2)}, u32[]{:S(2)}) collective-permute-start(f32[1,4096]{1,0:T(1,128)S(1)} %add.95), channel_id=1, source_target_pairs={{0,64},{64,0},{128,192},{192,128},{256,320},{320,256},{384,448},{4... | collective-permute-start | bytes 49160 | tf_op jit(solution)/shard_map/ppermute | solution.py:89
  56.0 2.1 %collective-permute-start.4 = (bf16[128,4096]{1,0:T(8,128)(2,1)S(1)}, bf16[128,4096]{1,0:T(8,128)(2,1)S(1)}, u32[]{:S(2)}, u32[]{:S(2)}) collective-permute-start(bf16[128,4096]{1,0:T(8,128)(2,1)S(1)} %bitcast.80), channel_id=1, source_target_pairs={{0,1},{1,0},{2,3},{3,2},{4,5},{5,4},{6,7},{7,6},{8,9},{9,8},{10,11... | collective-permute-start | bytes 3145736 | tf_op jit(solution)/shard_map/ppermute | solution.py:84
  58.1 1.3 collective-permute-done.3
  62.1 11.9 %collective-permute-start.5 = (bf16[256,128]{1,0:T(8,128)(2,1)S(1)}, bf16[256,128]{1,0:T(8,128)(2,1)S(1)}, u32[]{:S(2)}, u32[]{:S(2)}) collective-permute-start(bf16[256,128]{1,0:T(8,128)(2,1)S(1)} %bitcast.86), channel_id=1, source_target_pairs={{0,2},{2,0},{1,3},{3,1},{4,6},{6,4},{5,7},{7,5},{8,10},{10,8},{9,1... | collective-permute-start | bytes 196616 | tf_op jit(solution)/shard_map/ppermute | solution.py:112
  74.2 3.0 %collective-permute-done.5 = bf16[256,128]{1,0:T(8,128)(2,1)S(1)} collective-permute-done((bf16[256,128]{1,0:T(8,128)(2,1)S(1)}, bf16[256,128]{1,0:T(8,128)(2,1)S(1)}, u32[]{:S(2)}, u32[]{:S(2)}) %collective-permute-start.5) | collective-permute-done | bytes 65568 | tf_op jit(solution)/shard_map/ppermute | solution.py:112
  77.2 2.0 %all-gather = bf16[512,256]{1,0:T(8,128)(2,1)S(1)} all-gather(bf16[256,256]{1,0:T(8,128)(2,1)S(1)} %pad_maximum_fusion), channel_id=2, replica_groups=mesh['branch'=8,'x'=4,'y'=4,'zh'=2,'core'=2] {'core'}, dimensions={0}, use_global_device_ids=true | all-gather | bytes 393216 | tf_op jit(solution)/shard_map/all_gather | solution.py:116
  80.5 7.4 %all-to-all-start.2 = ((bf16[16,16,1024]{2,1,0:T(8,128)(2,1)}), bf16[16,16,1024]{2,1,0:T(8,128)(2,1)S(1)}, u32[]{:S(2)}, u32[]{:S(2)}) async-start(bf16[16,16,1024]{2,1,0:T(8,128)(2,1)} %bitcast.26), calls=%async_computation.2 | async-start | bytes 1048576 | tf_op jit(solution)/shard_map/all_to_all | solution.py:137
  87.9 9.2 %collective-permute-start.7 = (bf16[64,1024]{1,0:T(8,128)(2,1)S(1)}, bf16[64,1024]{1,0:T(8,128)(2,1)S(1)}, u32[]{:S(2)}, u32[]{:S(2)}) collective-permute-start(bf16[64,1024]{1,0:T(8,128)(2,1)S(1)} %broadcast_select_fusion), channel_id=1, source_target_pairs={{0,256},{64,320},{128,384},{192,448},{256,0},{320,64},{384,128},{4... | collective-permute-start | bytes 393224 | tf_op jit(solution)/shard_map/ppermute | solution.py:133
  97.1 11.6 %collective-permute-done.7 = bf16[64,1024]{1,0:T(8,128)(2,1)S(1)} collective-permute-done((bf16[64,1024]{1,0:T(8,128)(2,1)S(1)}, bf16[64,1024]{1,0:T(8,128)(2,1)S(1)}, u32[]{:S(2)}, u32[]{:S(2)}) %collective-permute-start.7) | collective-permute-done | bytes 131104 | tf_op jit(solution)/shard_map/ppermute | solution.py:133
  109.0 1.9 %collective-permute-start.6 = (bf16[8,1024]{1,0:T(8,128)(2,1)S(1)}, bf16[8,1024]{1,0:T(8,128)(2,1)S(1)}, u32[]{:S(2)}, u32[]{:S(2)}) collective-permute-start(bf16[8,1024]{1,0:T(8,128)(2,1)S(1)} %broadcast_select_fusion.5), channel_id=1, source_target_pairs={{0,1},{1,0},{2,3},{3,2},{4,5},{5,4},{6,7},{7,6},{8,9},{9,8},{10,11... | collective-permute-start | bytes 49160 | tf_op jit(solution)/shard_map/ppermute | solution.py:141
  110.9 1.9 %collective-permute-start.8 = (f32[64,512]{1,0:T(8,128)S(1)}, f32[64,512]{1,0:T(8,128)S(1)}, u32[]{:S(2)}, u32[]{:S(2)}) collective-permute-start(f32[64,512]{1,0:T(8,128)S(1)} %slice_select_fusion), channel_id=1, source_target_pairs={{0,128},{64,192},{128,0},{192,64},{256,384},{320,448},{384,256},{4... | collective-permute-start | bytes 393224 | tf_op jit(solution)/shard_map/ppermute | solution.py:133
  114.1 10.5 %all-to-all-start.3 = ((bf16[16,4,2048]{2,1,0:T(4,128)(2,1)}), bf16[16,4,2048]{2,1,0:T(4,128)(2,1)S(1)}, u32[]{:S(2)}, u32[]{:S(2)}) async-start(bf16[16,4,2048]{2,1,0:T(4,128)(2,1)} %bitcast.27), calls=%async_computation.3 | async-start | bytes 524288 | tf_op jit(solution)/shard_map/all_to_all | solution.py:153
  124.7 3.8 %collective-permute-start.9 = (f32[64,256]{1,0:T(8,128)S(1)}, f32[64,256]{1,0:T(8,128)S(1)}, u32[]{:S(2)}, u32[]{:S(2)}) collective-permute-start(f32[64,256]{1,0:T(8,128)S(1)} %slice_select_fusion.1), channel_id=1, source_target_pairs={{0,64},{64,0},{128,192},{192,128},{256,320},{320,256},{384,448},{4... | collective-permute-start | bytes 196616 | tf_op jit(solution)/shard_map/ppermute | solution.py:133
  128.6 9.4 %collective-permute-done.9 = f32[64,256]{1,0:T(8,128)S(1)} collective-permute-done((f32[64,256]{1,0:T(8,128)S(1)}, f32[64,256]{1,0:T(8,128)S(1)}, u32[]{:S(2)}, u32[]{:S(2)}) %collective-permute-start.9) | collective-permute-done | bytes 65568 | tf_op jit(solution)/shard_map/ppermute | solution.py:133
  138.6 8.8 %all-to-all-done.3 = bf16[16,4,2048]{2,1,0:T(4,128)(2,1)S(1)} async-done(((bf16[16,4,2048]{2,1,0:T(4,128)(2,1)}), bf16[16,4,2048]{2,1,0:T(4,128)(2,1)S(1)}, u32[]{:S(2)}, u32[]{:S(2)}) %all-to-all-start.3) | async-done | bytes 262176 | tf_op jit(solution)/shard_map/all_to_all | solution.py:153
  (80 shorter events, 10.9 us)
Async XLA Ops:
  0.6 59.6 %copy-start = (bf16[1,4096,128]{2,1,0:T(8,128)(2,1)S(1)}, bf16[1,4096,128]{2,1,0:T(8,128)(2,1)}, u32[]{:S(2)}) copy-start(bf16[1,4096,128]{2,1,0:T(8,128)(2,1)} %param.14) | copy-start | bytes 3145732
  0.6 1.3 copy-start.1
  3.0 9.6 %copy-start.5 = (s32[8,2]{0,1:T(2,128)S(1)}, s32[8,2]{0,1:T(2,128)}, u32[]{:S(2)}) copy-start(s32[8,2]{0,1:T(2,128)} %param.9) | copy-start | bytes 196
  3.0 10.0 %copy-start.3 = (bf16[8,4096]{1,0:T(8,128)(2,1)S(1)}, bf16[8,4096]{1,0:T(8,128)(2,1)}, u32[]{:S(2)}) copy-start(bf16[8,4096]{1,0:T(8,128)(2,1)} %param.8) | copy-start | bytes 196612
  3.0 26.1 %all-to-all-start = ((bf16[16,64,512]{2,1,0:T(8,128)(2,1)}), bf16[16,64,512]{2,1,0:T(8,128)(2,1)S(1)}, u32[]{:S(2)}, u32[]{:S(2)}) async-start(bf16[16,64,512]{2,1,0:T(8,128)(2,1)} %split_columns.1), calls=%async_computation | async-start | bytes 2097152 | tf_op jit(solution)/shard_map/all_to_all | solution.py:61
  13.3 15.8 %collective-permute-start = (bf16[8,4096]{1,0:T(8,128)(2,1)S(1)}, bf16[8,4096]{1,0:T(8,128)(2,1)S(1)}, u32[]{:S(2)}, u32[]{:S(2)}) collective-permute-start(bf16[8,4096]{1,0:T(8,128)(2,1)S(1)} %slice.65), channel_id=1, source_target_pairs={{0,258},{2,256},{64,322},{66,320},{128,386},{130,384},{192,450},{1... | collective-permute-start | bytes 196616 | tf_op jit(solution)/shard_map/ppermute | solution.py:79
  30.2 7.4 %copy-start.4 = (f32[1,4096]{1,0:T(1,128)S(1)}, f32[1,4096]{1,0:T(1,128)}, u32[]{:S(2)}) copy-start(f32[1,4096]{1,0:T(1,128)} %param.11) | copy-start | bytes 49156
  30.2 25.7 %all-to-all-start.1 = ((bf16[16,8,4096]{2,1,0:T(8,128)(2,1)}), bf16[16,8,4096]{2,1,0:T(8,128)(2,1)S(1)}, u32[]{:S(2)}, u32[]{:S(2)}) async-start(bf16[16,8,4096]{2,1,0:T(8,128)(2,1)} %broadcast_in_dim.30), calls=%async_computation.1 | async-start | bytes 2097152 | tf_op jit(solution)/shard_map/all_to_all | solution.py:83
  37.6 9.6 %collective-permute-start.1 = (f32[1,4096]{1,0:T(1,128)S(1)}, f32[1,4096]{1,0:T(1,128)S(1)}, u32[]{:S(2)}, u32[]{:S(2)}) collective-permute-start(f32[1,4096]{1,0:T(1,128)S(1)} %copy-done.4), channel_id=1, source_target_pairs={{0,256},{64,320},{128,384},{192,448},{256,0},{320,64},{384,128},{4... | collective-permute-start | bytes 49160 | tf_op jit(solution)/shard_map/ppermute | solution.py:89
  47.2 6.5 %collective-permute-start.2 = (f32[1,4096]{1,0:T(1,128)S(1)}, f32[1,4096]{1,0:T(1,128)S(1)}, u32[]{:S(2)}, u32[]{:S(2)}) collective-permute-start(f32[1,4096]{1,0:T(1,128)S(1)} %add.94), channel_id=1, source_target_pairs={{0,128},{64,192},{128,0},{192,64},{256,384},{320,448},{384,256},{4... | collective-permute-start | bytes 49160 | tf_op jit(solution)/shard_map/ppermute | solution.py:89
  53.7 5.6 %collective-permute-start.3 = (f32[1,4096]{1,0:T(1,128)S(1)}, f32[1,4096]{1,0:T(1,128)S(1)}, u32[]{:S(2)}, u32[]{:S(2)}) collective-permute-start(f32[1,4096]{1,0:T(1,128)S(1)} %add.95), channel_id=1, source_target_pairs={{0,64},{64,0},{128,192},{192,128},{256,320},{320,256},{384,448},{4... | collective-permute-start | bytes 49160 | tf_op jit(solution)/shard_map/ppermute | solution.py:89
  56.0 3.7 %copy-start.7 = (bf16[1,4096,128]{2,1,0:T(8,128)(2,1)S(1)}, bf16[1,4096,128]{2,1,0:T(8,128)(2,1)}, u32[]{:S(2)}) copy-start(bf16[1,4096,128]{2,1,0:T(8,128)(2,1)} %param.13) | copy-start | bytes 3145732
  56.0 4.7 %collective-permute-start.4 = (bf16[128,4096]{1,0:T(8,128)(2,1)S(1)}, bf16[128,4096]{1,0:T(8,128)(2,1)S(1)}, u32[]{:S(2)}, u32[]{:S(2)}) collective-permute-start(bf16[128,4096]{1,0:T(8,128)(2,1)S(1)} %bitcast.80), channel_id=1, source_target_pairs={{0,1},{1,0},{2,3},{3,2},{4,5},{5,4},{6,7},{7,6},{8,9},{9,8},{10,11... | collective-permute-start | bytes 3145736 | tf_op jit(solution)/shard_map/ppermute | solution.py:84
  62.1 15.1 %collective-permute-start.5 = (bf16[256,128]{1,0:T(8,128)(2,1)S(1)}, bf16[256,128]{1,0:T(8,128)(2,1)S(1)}, u32[]{:S(2)}, u32[]{:S(2)}) collective-permute-start(bf16[256,128]{1,0:T(8,128)(2,1)S(1)} %bitcast.86), channel_id=1, source_target_pairs={{0,2},{2,0},{1,3},{3,1},{4,6},{6,4},{5,7},{7,5},{8,10},{10,8},{9,1... | collective-permute-start | bytes 196616 | tf_op jit(solution)/shard_map/ppermute | solution.py:112
  80.5 7.4 %copy-start.2 = (bf16[1,64,2048]{2,1,0:T(8,128)(2,1)S(1)}, bf16[1,64,2048]{2,1,0:T(8,128)(2,1)}, u32[]{:S(2)}) copy-start(bf16[1,64,2048]{2,1,0:T(8,128)(2,1)} %param.12) | copy-start | bytes 786436
  80.5 28.3 %all-to-all-start.2 = ((bf16[16,16,1024]{2,1,0:T(8,128)(2,1)}), bf16[16,16,1024]{2,1,0:T(8,128)(2,1)S(1)}, u32[]{:S(2)}, u32[]{:S(2)}) async-start(bf16[16,16,1024]{2,1,0:T(8,128)(2,1)} %bitcast.26), calls=%async_computation.2 | async-start | bytes 1048576 | tf_op jit(solution)/shard_map/all_to_all | solution.py:137
  87.9 20.9 %collective-permute-start.7 = (bf16[64,1024]{1,0:T(8,128)(2,1)S(1)}, bf16[64,1024]{1,0:T(8,128)(2,1)S(1)}, u32[]{:S(2)}, u32[]{:S(2)}) collective-permute-start(bf16[64,1024]{1,0:T(8,128)(2,1)S(1)} %broadcast_select_fusion), channel_id=1, source_target_pairs={{0,256},{64,320},{128,384},{192,448},{256,0},{320,64},{384,128},{4... | collective-permute-start | bytes 393224 | tf_op jit(solution)/shard_map/ppermute | solution.py:133
  109.0 3.9 %collective-permute-start.6 = (bf16[8,1024]{1,0:T(8,128)(2,1)S(1)}, bf16[8,1024]{1,0:T(8,128)(2,1)S(1)}, u32[]{:S(2)}, u32[]{:S(2)}) collective-permute-start(bf16[8,1024]{1,0:T(8,128)(2,1)S(1)} %broadcast_select_fusion.5), channel_id=1, source_target_pairs={{0,1},{1,0},{2,3},{3,2},{4,5},{5,4},{6,7},{7,6},{8,9},{9,8},{10,11... | collective-permute-start | bytes 49160 | tf_op jit(solution)/shard_map/ppermute | solution.py:141
  110.9 17.6 %copy-start.6 = (f32[8,2]{0,1:T(2,128)S(1)}, f32[8,2]{0,1:T(2,128)}, u32[]{:S(2)}) copy-start(f32[8,2]{0,1:T(2,128)} %param.10) | copy-start | bytes 196
  110.9 13.7 %collective-permute-start.8 = (f32[64,512]{1,0:T(8,128)S(1)}, f32[64,512]{1,0:T(8,128)S(1)}, u32[]{:S(2)}, u32[]{:S(2)}) collective-permute-start(f32[64,512]{1,0:T(8,128)S(1)} %slice_select_fusion), channel_id=1, source_target_pairs={{0,128},{64,192},{128,0},{192,64},{256,384},{320,448},{384,256},{4... | collective-permute-start | bytes 393224 | tf_op jit(solution)/shard_map/ppermute | solution.py:133
  114.1 33.3 %all-to-all-start.3 = ((bf16[16,4,2048]{2,1,0:T(4,128)(2,1)}), bf16[16,4,2048]{2,1,0:T(4,128)(2,1)S(1)}, u32[]{:S(2)}, u32[]{:S(2)}) async-start(bf16[16,4,2048]{2,1,0:T(4,128)(2,1)} %bitcast.27), calls=%async_computation.3 | async-start | bytes 524288 | tf_op jit(solution)/shard_map/all_to_all | solution.py:153
  124.7 13.3 %collective-permute-start.9 = (f32[64,256]{1,0:T(8,128)S(1)}, f32[64,256]{1,0:T(8,128)S(1)}, u32[]{:S(2)}, u32[]{:S(2)}) collective-permute-start(f32[64,256]{1,0:T(8,128)S(1)} %slice_select_fusion.1), channel_id=1, source_target_pairs={{0,64},{64,0},{128,192},{192,128},{256,320},{320,256},{384,448},{4... | collective-permute-start | bytes 196616 | tf_op jit(solution)/shard_map/ppermute | solution.py:133

commit v4 on v3

v4 whole, which is shorter than its diff:
```python
import functools

import jax
import jax.numpy as jnp
from jax import lax
from jax.experimental import pallas as pl
from jax.experimental.pallas import tpu as pltpu
from jax.sharding import Mesh, PartitionSpec as P

F32 = jnp.float32
BF16 = jnp.bfloat16
XY = ("x", "y")
ZLINE = ("branch", "zh")
DP = ("x", "y", "zh", "core")
FLIP = [(0, 1), (1, 0)]


def split_kernel(parts, source, target):
    span = source.shape[1] // parts
    for part in range(parts):
        target[part] = source[:, part * span : (part + 1) * span]


def split_columns(array, parts):
    rows, cols = array.shape
    return pl.pallas_call(
        functools.partial(split_kernel, parts),
        out_shape=jax.ShapeDtypeStruct((parts, rows, cols // parts), array.dtype),
        cost_estimate=pl.CostEstimate(
            flops=0, bytes_accessed=4 * rows * cols, transcendentals=0
        ),
        compiler_params=pltpu.CompilerParams(vmem_limit_bytes=8 << 20),
        name="split_columns",
    )(array)


def pick_table(route_pair, wanted, wanted_slot):
    chosen = (route_pair[0:1, :] == wanted) | (route_pair[1:2, :] == wanted)
    toks = route_pair.shape[1]
    earlier = (
        lax.broadcasted_iota(jnp.int32, (toks, toks), 0)
        <= lax.broadcasted_iota(jnp.int32, (toks, toks), 1)
    ).astype(F32)
    count = jnp.dot(chosen.astype(F32), earlier, preferred_element_type=F32)
    return chosen & (count == (wanted_slot + 1).astype(F32))


def pack_kernel(experts, cap, tokens, route_pair, own, send):
    group = 2 * cap
    toks = tokens.shape[0]
    expert = lax.axis_index("branch")
    half = lax.axis_index("zh")
    row = lax.broadcasted_iota(jnp.int32, (2 * group, toks), 0)
    wanted = jnp.where(row < group, expert, lax.rem(expert + experts // 2, experts))
    here = (row >= group) | (row // cap == half)
    picks = pick_table(route_pair[...], wanted, lax.rem(row, cap)) & here
    packed = jnp.dot(picks.astype(BF16), tokens[...], preferred_element_type=F32)
    own[...] = packed[:group].astype(BF16)
    send[...] = packed[group : group + cap].astype(BF16)


def pack_rows(experts, cap, tokens, route_pair):
    group, width = 2 * cap, tokens.shape[1]
    return pl.pallas_call(
        functools.partial(pack_kernel, experts, cap),
        out_shape=(
            jax.ShapeDtypeStruct((group, width), BF16),
            jax.ShapeDtypeStruct((cap, width), BF16),
        ),
        cost_estimate=pl.CostEstimate(flops=1 << 20, bytes_accessed=1 << 18, transcendentals=0),
        compiler_params=pltpu.CompilerParams(vmem_limit_bytes=8 << 20),
        name="pack_rows",
    )(tokens, route_pair)


def hidden_kernel(inv_width, experts, mine, theirs, gain, gate, up, hidden, sums, gates, ups):
    step = pl.program_id(0)
    rows = mine.shape[0]

    @pl.when(step == 0)
    def _():
        sums[...] = jnp.zeros_like(sums)
        gates[...] = jnp.zeros_like(gates)
        ups[...] = jnp.zeros_like(ups)

    scale = gain[...] * (1.0 / experts)
    block = jnp.concatenate([mine[...], theirs[...]], axis=0).astype(F32)
    sums[...] += jnp.sum(block * block, axis=1, keepdims=True)
    scaled = (block * scale).astype(BF16)
    gates[...] += jnp.dot(scaled, gate[...], preferred_element_type=F32)
    ups[...] += jnp.dot(scaled, up[...], preferred_element_type=F32)

    @pl.when(step == pl.num_programs(0) - 1)
    def _():
        core = lax.axis_index("core")
        inv_rms = lax.rsqrt(sums[...] * inv_width + 1e-05)
        gate_part = gates[...] * inv_rms
        value = gate_part / (1.0 + jnp.exp(-gate_part)) * (ups[...] * inv_rms)
        value = value.astype(BF16)
        shape = (hidden.shape[0], hidden.shape[2], hidden.shape[3])
        hidden[:, core] = value[:rows].reshape(shape)
        hidden[:, 1 - core] = value[rows:].reshape(shape)


def hidden_units(experts, n_xy, mine, theirs, gain, gate, up, parts=4):
    rows, width = mine.shape
    units = gate.shape[1]
    span = width // parts
    return pl.pallas_call(
        functools.partial(hidden_kernel, 1.0 / width, experts),
        out_shape=jax.ShapeDtypeStruct((n_xy, 2, rows // n_xy, units), BF16),
        grid=(parts,),
        in_specs=[
            pl.BlockSpec((rows, span), lambda k: (0, k)),
            pl.BlockSpec((rows, span), lambda k: (0, k)),
            pl.BlockSpec((1, span), lambda k: (0, k)),
            pl.BlockSpec((span, units), lambda k: (k, 0)),
            pl.BlockSpec((span, units), lambda k: (k, 0)),
        ],
        out_specs=pl.BlockSpec((n_xy, 2, rows // n_xy, units), lambda k: (0, 0, 0, 0)),
        scratch_shapes=[
            pltpu.VMEM((2 * rows, 1), F32),
            pltpu.VMEM((2 * rows, units), F32),
            pltpu.VMEM((2 * rows, units), F32),
        ],
        cost_estimate=pl.CostEstimate(
            flops=8 * rows * width * units, bytes_accessed=1 << 22, transcendentals=1 << 16
        ),
        compiler_params=pltpu.CompilerParams(
            dimension_semantics=("arbitrary",), vmem_limit_bytes=8 << 20
        ),
        name="hidden_units",
    )(mine, theirs, gain, gate, up)


def fan_kernel(cap, total, fan):
    core = lax.axis_index("core")
    group = 2 * cap
    start = pl.multiple_of(core * group, group)
    left = total[0, pl.ds(start, group), :].astype(F32)
    right = total[1, pl.ds(start, group), :].astype(F32)
    line = lax.broadcasted_iota(jnp.int32, left.shape, 0)
    low = jnp.where(line < cap, left, pltpu.roll(right, cap, 0)).astype(BF16)
    high = jnp.where(line < cap, pltpu.roll(left, cap, 0), right).astype(BF16)
    for place in range(fan.shape[0] // 2):
        fan[2 * place] = low
        fan[2 * place + 1] = high


def fan_out(experts, cap, total):
    return pl.pallas_call(
        functools.partial(fan_kernel, cap),
        out_shape=jax.ShapeDtypeStruct((2 * experts, 2 * cap, total.shape[2]), BF16),
        cost_estimate=pl.CostEstimate(flops=1 << 16, bytes_accessed=1 << 19, transcendentals=0),
        compiler_params=pltpu.CompilerParams(vmem_limit_bytes=8 << 20),
        name="fan_out",
    )(total)


def mix_kernel(experts, cap, cols, tokens, route_pair, weight_pair, slots, mixed):
    toks = tokens.shape[0]
    group = 2 * cap
    keys = experts * group
    row = lax.broadcasted_iota(jnp.int32, (keys, toks), 0)
    wanted = row // group
    pair = route_pair[...]
    weights = weight_pair[...]
    picks = pick_table(pair, wanted, lax.rem(row, cap))
    share = jnp.where(pair[0:1, :] == wanted, weights[0:1, :], 0.0) + jnp.where(
        pair[1:2, :] == wanted, weights[1:2, :], 0.0
    )
    share = jnp.where(picks, share, 0.0)
    side = lax.rem(row // cap, 2)
    span = slots.shape[3]
    for half in range(2):
        rows = slots[:, half].astype(F32).reshape(keys, span)
        parts = [
            lax.dot_general(
                jnp.where(side == core, share, 0.0),
                rows,
                (((0,), (0,)), ((), ())),
                precision=lax.Precision.HIGHEST,
                preferred_element_type=F32,
            )
            for core in range(2)
        ]
        for block in range(span // cols):
            base = (block * 4 + half * 2) * cols
            cut = slice(block * cols, (block + 1) * cols)
            moe = jnp.concatenate([parts[0][:, cut], parts[1][:, cut]], axis=1)
            place = slice(base, base + 2 * cols)
            mixed[:, place] = (tokens[:, place].astype(F32) + moe).astype(BF16)


def mix_tokens(experts, cap, cols, tokens, route_pair, weight_pair, slots):
    return pl.pallas_call(
        functools.partial(mix_kernel, experts, cap, cols),
        out_shape=jax.ShapeDtypeStruct(tokens.shape, BF16),
        cost_estimate=pl.CostEstimate(flops=1 << 24, bytes_accessed=1 << 19, transcendentals=0),
        compiler_params=pltpu.CompilerParams(vmem_limit_bytes=8 << 20),
        name="mix_tokens",
    )(tokens, route_pair, weight_pair, slots)


def layer(
    tokens, routes, route_weights, norm_gains, keyval_weights, expert_gate, expert_up, expert_down
):
    experts = lax.axis_size("branch")
    n_xy = lax.axis_size("x") * lax.axis_size("y")
    expert = lax.axis_index("branch")
    half = lax.axis_index("zh")
    tok_count, width = tokens.shape
    cap = min(tok_count, 4 * tok_count // experts)
    group = 2 * cap
    steps = [experts >> shift for shift in range(1, experts.bit_length())]

    route_pair, weight_pair = routes.T, route_weights.T
    own, send = pack_rows(experts, cap, tokens, route_pair)
    swap = [
        (2 * e + z, 2 * ((e + experts // 2) % experts) + 1 - z)
        for e in range(experts)
        for z in range(2)
    ]
    arrived = lax.ppermute(send, ZLINE, swap)
    line = lax.broadcasted_iota(jnp.int32, own.shape, 0)
    both = jnp.where(line // cap == half, own, jnp.concatenate([arrived, arrived], axis=0))
    spread = jnp.broadcast_to(both[None], (n_xy, group, width))
    mine = lax.all_to_all(spread, XY, 0, 0, tiled=True).reshape(n_xy * group, width)
    theirs = lax.ppermute(mine, "core", FLIP)

    gain_sum = norm_gains
    for step in steps:
        came = lax.ppermute(gain_sum, "branch", [(b, b ^ step) for b in range(experts)])
        if step == steps[0]:
            came, _ = lax.optimization_barrier((came, spread))
        gain_sum = gain_sum + came

    down, _ = lax.optimization_barrier((expert_down[0].T, spread))
    cols = down.shape[0]
    down = split_columns(down, n_xy)
    down = lax.all_to_all(down, XY, 0, 0, tiled=True).reshape(n_xy * cols, -1)

    hid = hidden_units(experts, n_xy, mine, theirs, gain_sum, expert_gate[0], expert_up[0])
    units = hid.shape[3]
    hid = hid.reshape(2 * n_xy * group, units)
    hid_far = lax.ppermute(hid, "zh", FLIP)
    near = jnp.concatenate(
        [jnp.where(half == 0, hid, hid_far), jnp.where(half == 0, hid_far, hid)], axis=1
    )
    near = lax.all_gather(near, "core", axis=0, tiled=False)
    near = jnp.concatenate(
        [near[0, :, :units], near[1, :, :units], near[0, :, units:], near[1, :, units:]], axis=1
    )

    part = lax.dot_general(
        near, down, (((1,), (1,)), ((), ())), preferred_element_type=F32
    ).astype(BF16)
    part = part.reshape(n_xy, 2 * group, n_xy * cols)

    acc, _ = lax.optimization_barrier((keyval_weights[0], send))
    until = dict(zip(steps, (hid, part, part)))
    for step in steps:
        span = acc.shape[1] // 2
        upper = (expert // step) % 2 == 1
        stay = jnp.where(upper, acc[:, span:], acc[:, :span])
        leave = jnp.where(upper, acc[:, :span], acc[:, span:])
        came = lax.ppermute(leave, "branch", [(b, b ^ step) for b in range(experts)])
        came, _ = lax.optimization_barrier((came, until[step]))
        acc = stay.astype(F32) + came.astype(F32)

    part = lax.all_to_all(part, XY, 0, 0, tiled=True)
    total = jnp.sum(part.astype(F32), axis=0).astype(BF16)
    total = lax.all_gather(total, "core", axis=0, tiled=False)
    spread = fan_out(experts, cap, total)
    slots = lax.all_to_all(spread, ZLINE, 0, 0, tiled=True)
    slots = slots.reshape(experts, 2, group, n_xy * cols)
    acc, _ = lax.optimization_barrier((acc, spread))
    merged_keyval = (acc / experts).astype(BF16)
    mixed = mix_tokens(experts, cap, cols, tokens, route_pair, weight_pair, slots)
    return mixed, merged_keyval


def solution(mesh):
    n_x = n_y = int(round((mesh.devices.shape[1] // 4) ** 0.5))
    fine = Mesh(
        mesh.devices.reshape(mesh.devices.shape[0], n_x, n_y, 2, 2),
        ("branch", "x", "y", "zh", "core"),
    )
    in_specs = (
        P(DP, None),
        P(DP, None),
        P(DP, None),
        P("branch", None),
        P("branch", DP, None),
        P("branch", None, DP),
        P("branch", None, DP),
        P("branch", None, DP),
    )
    out_specs = (P(DP, None), P(DP, "branch"))
    return jax.shard_map(layer, mesh=fine, in_specs=in_specs, out_specs=out_specs, check_vma=False)
```

time: 150 us -> 150 us (level)
  blocking collectives: 1.99 us -> 24.9 us
  starting transfers between devices: 87.6 us -> 67.4 us
  Pallas kernels: 1.04 us -> 6.93 us
  waiting for transfers between devices: 46.2 us -> 40.4 us
  local copies, waits for them, and re-layouts: 4.21 us -> 2.36 us
  matrix products: 4.15 us -> 2.5 us
    all_to_all x0 -> x1, blocking collectives: none -> 21 us  [layer(): lax.all_to_all(spread, XY, 0, 0, tiled=True).reshape(n_xy * group, width)]
    ppermute x8 -> x7, waiting for transfers between devices: 34.4 us -> 16.5 us  [the longest x3 9.6 us: layer(): lax.ppermute(leave, 'branch', [(b, b ^ step) for b in range(experts)])]
    all_to_all x1 -> x0, starting transfers between devices: 7.36 us -> none  [layer(): lax.all_to_all(spread, XY, 0, 0, tiled=True).reshape(n_xy * group, width)]
    all_to_all x1, waiting for transfers between devices: 0.01 us -> 6.84 us  [layer(): part = lax.all_to_all(part, XY, 0, 0, tiled=True)]
    pallas_call x0 -> x4, Pallas kernels: none -> 5.9 us  [the longest x1 3.48 us: hidden_units(): pl.pallas_call(functools.partial(hidden_kernel, 1.0 / width, experts), ou...]
    ppermute x1, waiting for transfers between devices: 2.99 us -> 8.27 us  [layer(): hid_far = lax.ppermute(hid, 'zh', FLIP)]
    ppermute x1, starting transfers between devices: 11.9 us -> 7.89 us  [layer(): hid_far = lax.ppermute(hid, 'zh', FLIP)]
    all_to_all x1, starting transfers between devices: 10.5 us -> 7.12 us  [layer(): slots = lax.all_to_all(spread, ZLINE, 0, 0, tiled=True)]
  transfers between devices with their start and end apart: 14 -> 12, of which waited for: 8 -> 7; matrix products, arithmetic and copies ran while one was open for 3% -> 2% of each run, Pallas kernels for 0% -> 4%
where the time goes in v4:
time: 150 us; the launch traced here: 148 us
  starting transfers between devices  67.4 us (45%)
  waiting for transfers between devices  40.4 us (27%)
  blocking collectives  24.9 us (17%)
  Pallas kernels  6.93 us (5%)
  other arithmetic  2.57 us (2%)
  matrix products  2.5 us (2%)
  local copies, waits for them, and re-layouts  2.36 us (2%)
    all_to_all x1, blocking collectives, layer(): lax.all_to_all(spread, XY, 0, 0, tiled=True).reshape(n_xy * group, width)  21 us
    ppermute x3, starting transfers between devices, layer(): lax.ppermute(leave, 'branch', [(b, b ^ step) for b in range(experts)])  12.8 us
    ppermute x1, starting transfers between devices, layer(): arrived = lax.ppermute(send, ZLINE, swap)  12.7 us
    ppermute x3, starting transfers between devices, layer(): lax.ppermute(gain_sum, 'branch', [(b, b ^ step) for b in range(experts)])  11.3 us
    ppermute x3, waiting for transfers between devices, layer(): lax.ppermute(leave, 'branch', [(b, b ^ step) for b in range(experts)])  9.6 us
    all_to_all x1, waiting for transfers between devices, layer(): slots = lax.all_to_all(spread, ZLINE, 0, 0, tiled=True)  8.73 us
    ppermute x1, waiting for transfers between devices, layer(): hid_far = lax.ppermute(hid, 'zh', FLIP)  8.27 us
    ppermute x1, starting transfers between devices, layer(): hid_far = lax.ppermute(hid, 'zh', FLIP)  7.89 us
  transfers between devices with their start and end apart: 12, of which 7 were waited for; matrix products, arithmetic and copies ran while one was open for 2% of the time, Pallas kernels for 4%

profile of v4, /device:TPU:6, one launch (start us, length us, event | category | flops | bytes accessed | tf_op | source)
XLA Modules:
  0.0 148.0 jit_solution(7336290979870075188)
XLA Ops:
  2.4 12.7 %collective-permute-start = (bf16[4,4096]{1,0:T(4,128)(2,1)S(1)}, bf16[4,4096]{1,0:T(4,128)(2,1)S(1)}, u32[]{:S(2)}, u32[]{:S(2)}) collective-permute-start(bf16[4,4096]{1,0:T(4,128)(2,1)S(1)} %get-tuple-element.12), channel_id=1, source_target_pairs={{0,258},{2,256},{64,322},{66,320},{128,386},{130,384},{192,450},{1... | collective-permute-start | bytes 98312 | tf_op jit(solution)/shard_map/ppermute | solution.py:224
  15.2 2.6 %collective-permute-done = bf16[4,4096]{1,0:T(4,128)(2,1)S(1)} collective-permute-done((bf16[4,4096]{1,0:T(4,128)(2,1)S(1)}, bf16[4,4096]{1,0:T(4,128)(2,1)S(1)}, u32[]{:S(2)}, u32[]{:S(2)}) %collective-permute-start) | collective-permute-done | bytes 32800 | tf_op jit(solution)/shard_map/ppermute | solution.py:224
  18.0 21.0 %all_to_all.20 = bf16[16,8,4096]{2,1,0:T(8,128)(2,1)S(1)} all-to-all(bf16[16,8,4096]{2,1,0:T(8,128)(2,1)S(1)} %broadcast_in_dim.2), channel_id=1, replica_groups=mesh['branch'=8,'x'=4,'y'=4,'zh'=2,'core'=2] {'x','y'}, dimensions={0} | all-to-all | bytes 2097152 | tf_op jit(solution)/shard_map/all_to_all | solution.py:228
  39.0 1.9 %collective-permute-start.1 = (bf16[128,4096]{1,0:T(8,128)(2,1)S(1)}, bf16[128,4096]{1,0:T(8,128)(2,1)}, u32[]{:S(2)}, u32[]{:S(2)}) collective-permute-start(bf16[128,4096]{1,0:T(8,128)(2,1)S(1)} %bitcast.26), channel_id=1, source_target_pairs={{0,1},{1,0},{2,3},{3,2},{4,5},{5,4},{6,7},{7,6},{8,9},{9,8},{10,11... | collective-permute-start | bytes 3145736 | tf_op jit(solution)/shard_map/ppermute | solution.py:229
  41.0 5.3 %collective-permute-start.2 = (f32[1,4096]{1,0:T(1,128)S(1)}, f32[1,4096]{1,0:T(1,128)S(1)}, u32[]{:S(2)}, u32[]{:S(2)}) collective-permute-start(f32[1,4096]{1,0:T(1,128)S(1)} %copy-done.8), channel_id=1, source_target_pairs={{0,256},{64,320},{128,384},{192,448},{256,0},{320,64},{384,128},{4... | collective-permute-start | bytes 49160 | tf_op jit(solution)/shard_map/ppermute | solution.py:233
  46.2 4.3 %collective-permute-done.2 = f32[1,4096]{1,0:T(1,128)S(1)} collective-permute-done((f32[1,4096]{1,0:T(1,128)S(1)}, f32[1,4096]{1,0:T(1,128)S(1)}, u32[]{:S(2)}, u32[]{:S(2)}) %collective-permute-start.2) | collective-permute-done | bytes 16416 | tf_op jit(solution)/shard_map/ppermute | solution.py:233
  50.6 3.3 %collective-permute-start.3 = (f32[1,4096]{1,0:T(1,128)S(1)}, f32[1,4096]{1,0:T(1,128)S(1)}, u32[]{:S(2)}, u32[]{:S(2)}) collective-permute-start(f32[1,4096]{1,0:T(1,128)S(1)} %add.33), channel_id=1, source_target_pairs={{0,128},{64,192},{128,0},{192,64},{256,384},{320,448},{384,256},{4... | collective-permute-start | bytes 49160 | tf_op jit(solution)/shard_map/ppermute | solution.py:233
  55.0 6.4 %all-to-all-start.1 = ((bf16[16,64,512]{2,1,0:T(8,128)(2,1)}), bf16[16,64,512]{2,1,0:T(8,128)(2,1)}, u32[]{:S(2)}, u32[]{:S(2)}) async-start(bf16[16,64,512]{2,1,0:T(8,128)(2,1)} %split_columns.1), calls=%async_computation.1 | async-start | bytes 2097152 | tf_op jit(solution)/shard_map/all_to_all | solution.py:241
  61.4 2.8 %collective-permute-start.4 = (f32[1,4096]{1,0:T(1,128)S(1)}, f32[1,4096]{1,0:T(1,128)S(1)}, u32[]{:S(2)}, u32[]{:S(2)}) collective-permute-start(f32[1,4096]{1,0:T(1,128)S(1)} %add.34), channel_id=1, source_target_pairs={{0,64},{64,0},{128,192},{192,128},{256,320},{320,256},{384,448},{4... | collective-permute-start | bytes 49160 | tf_op jit(solution)/shard_map/ppermute | solution.py:233
  64.8 7.1 %collective-permute-start.6 = (bf16[64,1024]{1,0:T(8,128)(2,1)}, bf16[64,1024]{1,0:T(8,128)(2,1)}, u32[]{:S(2)}, u32[]{:S(2)}) collective-permute-start(bf16[64,1024]{1,0:T(8,128)(2,1)} %broadcast_select_fusion), channel_id=1, source_target_pairs={{0,256},{64,320},{128,384},{192,448},{256,0},{320,64},{384,128},{4... | collective-permute-start | bytes 393224 | tf_op jit(solution)/shard_map/ppermute | solution.py:267
  72.0 3.5 %hidden_units.1 = bf16[16,2,8,128]{3,2,1,0:T(8,128)(2,1)S(1)} custom-call(bf16[128,4096]{1,0:T(8,128)(2,1)S(1)} %bitcast.27, bf16[128,4096]{1,0:T(8,128)(2,1)} %collective-permute-done.1.theirs, f32[1,4096]{1,0:T(1,128)S(1)} %add.35.gain, bf16[4096,128]{1,0:T(8,128)(2,1)S(1)} %bitcast.30, bf16[4096,128]{1,0:T(8,128)(2,1)S(1)} %bitcast.31), custom_call_target="tpu_custom_call" | custom-call | flops 536870912 | bytes 4194304 | tf_op jit(solution)/shard_map/hidden_units/pallas_call | solution.py:109
  75.5 7.9 %collective-permute-start.5 = (bf16[256,128]{1,0:T(8,128)(2,1)S(1)}, bf16[256,128]{1,0:T(8,128)(2,1)S(1)}, u32[]{:S(2)}, u32[]{:S(2)}) collective-permute-start(bf16[256,128]{1,0:T(8,128)(2,1)S(1)} %bitcast.32), channel_id=1, source_target_pairs={{0,2},{2,0},{1,3},{3,1},{4,6},{6,4},{5,7},{7,5},{8,10},{10,8},{9,1... | collective-permute-start | bytes 196616 | tf_op jit(solution)/shard_map/ppermute | solution.py:246
  83.6 8.3 %collective-permute-done.5 = bf16[256,128]{1,0:T(8,128)(2,1)S(1)} collective-permute-done((bf16[256,128]{1,0:T(8,128)(2,1)S(1)}, bf16[256,128]{1,0:T(8,128)(2,1)S(1)}, u32[]{:S(2)}, u32[]{:S(2)}) %collective-permute-start.5) | collective-permute-done | bytes 65568 | tf_op jit(solution)/shard_map/ppermute | solution.py:246
  91.9 2.0 %all-gather = bf16[512,256]{1,0:T(8,128)(2,1)S(1)} all-gather(bf16[256,256]{1,0:T(8,128)(2,1)S(1)} %pad_maximum_fusion), channel_id=2, replica_groups=mesh['branch'=8,'x'=4,'y'=4,'zh'=2,'core'=2] {'core'}, dimensions={0}, use_global_device_ids=true | all-gather | bytes 393216 | tf_op jit(solution)/shard_map/all_gather | solution.py:250
  94.0 2.5 %convolution_convert_fusion = bf16[256,1024]{1,0:T(8,128)(2,1)} fusion(bf16[1024,512]{1,0:T(8,128)(2,1)} %bitcast.13, bf16[256,128]{1,0:T(8,128)(2,1)S(1)} %get-tuple-element.21, bf16[256,128]{1,0:T(8,128)(2,1)S(1)} %get-tuple-element.22, bf16[256,128]{1,0:T(8,128)(2,1)S(1)} %get-tuple-element.23, bf16[256,128]{1,0:T(8,128)(2,1)S(1)} %get-tuple-element.20), kind=kOutput, calls=%fused_computation | convolution fusion | flops 269746176 | bytes 1835008 | tf_op jit(solution)/shard_map/dot_general | solution.py:255
  96.5 7.2 %all-to-all-start.2 = ((bf16[16,16,1024]{2,1,0:T(8,128)(2,1)}), bf16[16,16,1024]{2,1,0:T(8,128)(2,1)S(1)}, u32[]{:S(2)}, u32[]{:S(2)}) async-start(bf16[16,16,1024]{2,1,0:T(8,128)(2,1)} %bitcast.14), calls=%async_computation.2 | async-start | bytes 1048576 | tf_op jit(solution)/shard_map/all_to_all | solution.py:271
  104.7 1.9 %collective-permute-start.7 = (f32[64,512]{1,0:T(8,128)S(1)}, f32[64,512]{1,0:T(8,128)S(1)}, u32[]{:S(2)}, u32[]{:S(2)}) collective-permute-start(f32[64,512]{1,0:T(8,128)S(1)} %slice_select_fusion), channel_id=1, source_target_pairs={{0,128},{64,192},{128,0},{192,64},{256,384},{320,448},{384,256},{4... | collective-permute-start | bytes 393224 | tf_op jit(solution)/shard_map/ppermute | solution.py:267
  106.6 6.8 %all-to-all-done.2 = bf16[16,16,1024]{2,1,0:T(8,128)(2,1)S(1)} async-done(((bf16[16,16,1024]{2,1,0:T(8,128)(2,1)}), bf16[16,16,1024]{2,1,0:T(8,128)(2,1)S(1)}, u32[]{:S(2)}, u32[]{:S(2)}) %all-to-all-start.2) | async-done | bytes 524320 | tf_op jit(solution)/shard_map/all_to_all | solution.py:271
  113.5 1.9 %all-gather.1 = bf16[32,1024]{1,0:T(8,128)(2,1)S(1)} all-gather(bf16[16,1024]{1,0:T(8,128)(2,1)S(1)} %reduce_sum.12), channel_id=3, replica_groups=mesh['branch'=8,'x'=4,'y'=4,'zh'=2,'core'=2] {'core'}, dimensions={0}, use_global_device_ids=true | all-gather | bytes 98304 | tf_op jit(solution)/shard_map/all_gather | solution.py:273
  116.1 7.1 %all-to-all-start.3 = ((bf16[16,8,1024]{2,1,0:T(8,128)(2,1)}), bf16[16,8,1024]{2,1,0:T(8,128)(2,1)S(1)}, u32[]{:S(2)}, u32[]{:S(2)}) async-start(bf16[16,8,1024]{2,1,0:T(8,128)(2,1)} %fan_out.1), calls=%async_computation.3 | async-start | bytes 524288 | tf_op jit(solution)/shard_map/all_to_all | solution.py:275
  123.3 3.8 %collective-permute-start.8 = (f32[64,256]{1,0:T(8,128)S(1)}, f32[64,256]{1,0:T(8,128)S(1)}, u32[]{:S(2)}, u32[]{:S(2)}) collective-permute-start(f32[64,256]{1,0:T(8,128)S(1)} %slice_select_fusion.1), channel_id=1, source_target_pairs={{0,64},{64,0},{128,192},{192,128},{256,320},{320,256},{384,448},{4... | collective-permute-start | bytes 196616 | tf_op jit(solution)/shard_map/ppermute | solution.py:267
  127.1 9.4 %collective-permute-done.8 = f32[64,256]{1,0:T(8,128)S(1)} collective-permute-done((f32[64,256]{1,0:T(8,128)S(1)}, f32[64,256]{1,0:T(8,128)S(1)}, u32[]{:S(2)}, u32[]{:S(2)}) %collective-permute-start.8) | collective-permute-done | bytes 65568 | tf_op jit(solution)/shard_map/ppermute | solution.py:267
  137.2 8.7 %all-to-all-done.3 = bf16[16,8,1024]{2,1,0:T(8,128)(2,1)S(1)} async-done(((bf16[16,8,1024]{2,1,0:T(8,128)(2,1)}), bf16[16,8,1024]{2,1,0:T(8,128)(2,1)S(1)}, u32[]{:S(2)}, u32[]{:S(2)}) %all-to-all-start.3) | async-done | bytes 262176 | tf_op jit(solution)/shard_map/all_to_all | solution.py:275
  146.6 1.4 mix_tokens.1
  (45 shorter events, 7.2 us)
Async XLA Ops:
  0.6 0.7 copy-start.5
  1.3 0.8 copy-start.3
  2.4 15.4 %collective-permute-start = (bf16[4,4096]{1,0:T(4,128)(2,1)S(1)}, bf16[4,4096]{1,0:T(4,128)(2,1)S(1)}, u32[]{:S(2)}, u32[]{:S(2)}) collective-permute-start(bf16[4,4096]{1,0:T(4,128)(2,1)S(1)} %get-tuple-element.12), channel_id=1, source_target_pairs={{0,258},{2,256},{64,322},{66,320},{128,386},{130,384},{192,450},{1... | collective-permute-start | bytes 98312 | tf_op jit(solution)/shard_map/ppermute | solution.py:224
  18.0 23.0 %copy-start.8 = (f32[1,4096]{1,0:T(1,128)S(1)}, f32[1,4096]{1,0:T(1,128)}, u32[]{:S(2)}) copy-start(f32[1,4096]{1,0:T(1,128)} %param.11) | copy-start | bytes 49156
  18.0 35.9 %copy-start = (bf16[1,8192,64]{1,2,0:T(8,128)(2,1)S(1)}, bf16[1,8192,64]{1,2,0:T(8,128)(2,1)}, u32[]{:S(2)}) copy-start(bf16[1,8192,64]{1,2,0:T(8,128)(2,1)} %param.15) | copy-start | bytes 3145732
  39.0 32.9 %collective-permute-start.1 = (bf16[128,4096]{1,0:T(8,128)(2,1)S(1)}, bf16[128,4096]{1,0:T(8,128)(2,1)}, u32[]{:S(2)}, u32[]{:S(2)}) collective-permute-start(bf16[128,4096]{1,0:T(8,128)(2,1)S(1)} %bitcast.26), channel_id=1, source_target_pairs={{0,1},{1,0},{2,3},{3,2},{4,5},{5,4},{6,7},{7,6},{8,9},{9,8},{10,11... | collective-permute-start | bytes 3145736 | tf_op jit(solution)/shard_map/ppermute | solution.py:229
  41.0 9.6 %collective-permute-start.2 = (f32[1,4096]{1,0:T(1,128)S(1)}, f32[1,4096]{1,0:T(1,128)S(1)}, u32[]{:S(2)}, u32[]{:S(2)}) collective-permute-start(f32[1,4096]{1,0:T(1,128)S(1)} %copy-done.8), channel_id=1, source_target_pairs={{0,256},{64,320},{128,384},{192,448},{256,0},{320,64},{384,128},{4... | collective-permute-start | bytes 49160 | tf_op jit(solution)/shard_map/ppermute | solution.py:233
  50.6 10.8 %collective-permute-start.3 = (f32[1,4096]{1,0:T(1,128)S(1)}, f32[1,4096]{1,0:T(1,128)S(1)}, u32[]{:S(2)}, u32[]{:S(2)}) collective-permute-start(f32[1,4096]{1,0:T(1,128)S(1)} %add.33), channel_id=1, source_target_pairs={{0,128},{64,192},{128,0},{192,64},{256,384},{320,448},{384,256},{4... | collective-permute-start | bytes 49160 | tf_op jit(solution)/shard_map/ppermute | solution.py:233
  53.9 10.3 %copy-start.7 = (bf16[1,64,2048]{2,1,0:T(8,128)(2,1)S(1)}, bf16[1,64,2048]{2,1,0:T(8,128)(2,1)}, u32[]{:S(2)}) copy-start(bf16[1,64,2048]{2,1,0:T(8,128)(2,1)} %param.12) | copy-start | bytes 786436
  55.0 17.0 %copy-start.1 = (bf16[1,4096,128]{2,1,0:T(8,128)(2,1)S(1)}, bf16[1,4096,128]{2,1,0:T(8,128)(2,1)}, u32[]{:S(2)}) copy-start(bf16[1,4096,128]{2,1,0:T(8,128)(2,1)} %param.13) | copy-start | bytes 3145732
  55.0 17.0 %copy-start.2 = (bf16[1,4096,128]{2,1,0:T(8,128)(2,1)S(1)}, bf16[1,4096,128]{2,1,0:T(8,128)(2,1)}, u32[]{:S(2)}) copy-start(bf16[1,4096,128]{2,1,0:T(8,128)(2,1)} %param.14) | copy-start | bytes 3145732
  55.0 39.0 %all-to-all-start.1 = ((bf16[16,64,512]{2,1,0:T(8,128)(2,1)}), bf16[16,64,512]{2,1,0:T(8,128)(2,1)}, u32[]{:S(2)}, u32[]{:S(2)}) async-start(bf16[16,64,512]{2,1,0:T(8,128)(2,1)} %split_columns.1), calls=%async_computation.1 | async-start | bytes 2097152 | tf_op jit(solution)/shard_map/all_to_all | solution.py:241
  61.4 10.5 %collective-permute-start.4 = (f32[1,4096]{1,0:T(1,128)S(1)}, f32[1,4096]{1,0:T(1,128)S(1)}, u32[]{:S(2)}, u32[]{:S(2)}) collective-permute-start(f32[1,4096]{1,0:T(1,128)S(1)} %add.34), channel_id=1, source_target_pairs={{0,64},{64,0},{128,192},{192,128},{256,320},{320,256},{384,448},{4... | collective-permute-start | bytes 49160 | tf_op jit(solution)/shard_map/ppermute | solution.py:233
  64.8 18.8 %collective-permute-start.6 = (bf16[64,1024]{1,0:T(8,128)(2,1)}, bf16[64,1024]{1,0:T(8,128)(2,1)}, u32[]{:S(2)}, u32[]{:S(2)}) collective-permute-start(bf16[64,1024]{1,0:T(8,128)(2,1)} %broadcast_select_fusion), channel_id=1, source_target_pairs={{0,256},{64,320},{128,384},{192,448},{256,0},{320,64},{384,128},{4... | collective-permute-start | bytes 393224 | tf_op jit(solution)/shard_map/ppermute | solution.py:267
  75.5 16.4 %collective-permute-start.5 = (bf16[256,128]{1,0:T(8,128)(2,1)S(1)}, bf16[256,128]{1,0:T(8,128)(2,1)S(1)}, u32[]{:S(2)}, u32[]{:S(2)}) collective-permute-start(bf16[256,128]{1,0:T(8,128)(2,1)S(1)} %bitcast.32), channel_id=1, source_target_pairs={{0,2},{2,0},{1,3},{3,1},{4,6},{6,4},{5,7},{7,5},{8,10},{10,8},{9,1... | collective-permute-start | bytes 196616 | tf_op jit(solution)/shard_map/ppermute | solution.py:246
  96.5 17.0 %all-to-all-start.2 = ((bf16[16,16,1024]{2,1,0:T(8,128)(2,1)}), bf16[16,16,1024]{2,1,0:T(8,128)(2,1)S(1)}, u32[]{:S(2)}, u32[]{:S(2)}) async-start(bf16[16,16,1024]{2,1,0:T(8,128)(2,1)} %bitcast.14), calls=%async_computation.2 | async-start | bytes 1048576 | tf_op jit(solution)/shard_map/all_to_all | solution.py:271
  104.7 18.6 %collective-permute-start.7 = (f32[64,512]{1,0:T(8,128)S(1)}, f32[64,512]{1,0:T(8,128)S(1)}, u32[]{:S(2)}, u32[]{:S(2)}) collective-permute-start(f32[64,512]{1,0:T(8,128)S(1)} %slice_select_fusion), channel_id=1, source_target_pairs={{0,128},{64,192},{128,0},{192,64},{256,384},{320,448},{384,256},{4... | collective-permute-start | bytes 393224 | tf_op jit(solution)/shard_map/ppermute | solution.py:267
  116.1 29.8 %all-to-all-start.3 = ((bf16[16,8,1024]{2,1,0:T(8,128)(2,1)}), bf16[16,8,1024]{2,1,0:T(8,128)(2,1)S(1)}, u32[]{:S(2)}, u32[]{:S(2)}) async-start(bf16[16,8,1024]{2,1,0:T(8,128)(2,1)} %fan_out.1), calls=%async_computation.3 | async-start | bytes 524288 | tf_op jit(solution)/shard_map/all_to_all | solution.py:275
  123.3 13.3 %collective-permute-start.8 = (f32[64,256]{1,0:T(8,128)S(1)}, f32[64,256]{1,0:T(8,128)S(1)}, u32[]{:S(2)}, u32[]{:S(2)}) collective-permute-start(f32[64,256]{1,0:T(8,128)S(1)} %slice_select_fusion.1), channel_id=1, source_target_pairs={{0,64},{64,0},{128,192},{192,128},{256,320},{320,256},{384,448},{4... | collective-permute-start | bytes 196616 | tf_op jit(solution)/shard_map/ppermute | solution.py:267
  136.6 9.4 %copy-start.4 = (bf16[8,4096]{1,0:T(8,128)(2,1)S(1)}, bf16[8,4096]{1,0:T(8,128)(2,1)}, u32[]{:S(2)}) copy-start(bf16[8,4096]{1,0:T(8,128)(2,1)} %tokens.3) | copy-start | bytes 196612
  145.9 0.7 copy-start.6

commit v5 on v4

--- a/solution.py
+++ b/solution.py
@@ -31,6 +31,33 @@
         ),
         compiler_params=pltpu.CompilerParams(vmem_limit_bytes=8 << 20),
         name="split_columns",
+    )(array)
+
+
+def stage_kernel(parts, source, target, sems):
+    span = target.shape[0] // parts
+    loads = [
+        pltpu.make_async_copy(
+            source.at[pl.ds(part * span, span)], target.at[pl.ds(part * span, span)], sems.at[part]
+        )
+        for part in range(parts)
+    ]
+    for load in loads:
+        load.start()
+    for load in loads:
+        load.wait()
+
+
+def stage(array, parts=4):
+    return pl.pallas_call(
+        functools.partial(stage_kernel, parts),
+        out_shape=jax.ShapeDtypeStruct(array.shape, array.dtype),
+        in_specs=[pl.BlockSpec(memory_space=pltpu.HBM)],
+        out_specs=pl.BlockSpec(memory_space=pltpu.VMEM),
+        scratch_shapes=[pltpu.SemaphoreType.DMA((parts,))],
+        cost_estimate=pl.CostEstimate(flops=0, bytes_accessed=2 * array.size, transcendentals=0),
+        compiler_params=pltpu.CompilerParams(vmem_limit_bytes=4 << 20),
+        name="stage",
     )(array)
 
 
@@ -73,62 +100,58 @@
     )(tokens, route_pair)
 
 
-def hidden_kernel(inv_width, experts, mine, theirs, gain, gate, up, hidden, sums, gates, ups):
-    step = pl.program_id(0)
-    rows = mine.shape[0]
-
-    @pl.when(step == 0)
-    def _():
-        sums[...] = jnp.zeros_like(sums)
-        gates[...] = jnp.zeros_like(gates)
-        ups[...] = jnp.zeros_like(ups)
-
-    scale = gain[...] * (1.0 / experts)
-    block = jnp.concatenate([mine[...], theirs[...]], axis=0).astype(F32)
-    sums[...] += jnp.sum(block * block, axis=1, keepdims=True)
-    scaled = (block * scale).astype(BF16)
-    gates[...] += jnp.dot(scaled, gate[...], preferred_element_type=F32)
-    ups[...] += jnp.dot(scaled, up[...], preferred_element_type=F32)
-
-    @pl.when(step == pl.num_programs(0) - 1)
-    def _():
-        core = lax.axis_index("core")
-        inv_rms = lax.rsqrt(sums[...] * inv_width + 1e-05)
-        gate_part = gates[...] * inv_rms
-        value = gate_part / (1.0 + jnp.exp(-gate_part)) * (ups[...] * inv_rms)
-        value = value.astype(BF16)
-        shape = (hidden.shape[0], hidden.shape[2], hidden.shape[3])
-        hidden[:, core] = value[:rows].reshape(shape)
-        hidden[:, 1 - core] = value[rows:].reshape(shape)
+def hidden_kernel(experts, parts, mine, theirs_hbm, gain, gate, up, hidden, theirs, sems):
+    _, width = mine.shape
+    span = width // parts
+    cuts = [slice(part * span, (part + 1) * span) for part in range(parts)]
+    loads = [
+        pltpu.make_async_copy(theirs_hbm.at[:, cut], theirs.at[:, cut], sems.at[part])
+        for part, cut in enumerate(cuts)
+    ]
+    for load in loads:
+        load.start()
+    sides = []
+    for source, waits in ((mine, ()), (theirs, loads)):
+        gate_part = up_part = total = None
+        for part, cut in enumerate(cuts):
+            if waits:
+                waits[part].wait()
+            scale = gain[:, cut] * (1.0 / experts)
+            block = source[:, cut].astype(F32)
+            square = jnp.sum(block * block, axis=1, keepdims=True)
+            scaled = (block * scale).astype(BF16)
+            gates = jnp.dot(scaled, gate[cut, :], preferred_element_type=F32)
+            ups = jnp.dot(scaled, up[cut, :], preferred_element_type=F32)
+            total = square if total is None else total + square
+            gate_part = gates if gate_part is None else gate_part + gates
+            up_part = ups if up_part is None else up_part + ups
+        inv_rms = lax.rsqrt(total * (1.0 / width) + 1e-05)
+        gate_part = gate_part * inv_rms
+        value = gate_part / (1.0 + jnp.exp(-gate_part)) * (up_part * inv_rms)
+        sides.append(value.astype(BF16))
+    core = lax.axis_index("core")
+    shape = (hidden.shape[0], hidden.shape[2], hidden.shape[3])
+    hidden[:, core] = sides[0].reshape(shape)
+    hidden[:, 1 - core] = sides[1].reshape(shape)
 
 
 def hidden_units(experts, n_xy, mine, theirs, gain, gate, up, parts=4):
     rows, width = mine.shape
     units = gate.shape[1]
-    span = width // parts
-    return pl.pallas_call(
-        functools.partial(hidden_kernel, 1.0 / width, experts),
+    whole = pl.BlockSpec(memory_space=pltpu.VMEM)
+    return pl.pallas_call(
+        functools.partial(hidden_kernel, experts, parts),
         out_shape=jax.ShapeDtypeStruct((n_xy, 2, rows // n_xy, units), BF16),
-        grid=(parts,),
-        in_specs=[
-            pl.BlockSpec((rows, span), lambda k: (0, k)),
-            pl.BlockSpec((rows, span), lambda k: (0, k)),
-            pl.BlockSpec((1, span), lambda k: (0, k)),
-            pl.BlockSpec((span, units), lambda k: (k, 0)),
-            pl.BlockSpec((span, units), lambda k: (k, 0)),
-        ],
-        out_specs=pl.BlockSpec((n_xy, 2, rows // n_xy, units), lambda k: (0, 0, 0, 0)),
+        in_specs=[whole, pl.BlockSpec(memory_space=pltpu.HBM), whole, whole, whole],
+        out_specs=whole,
         scratch_shapes=[
-            pltpu.VMEM((2 * rows, 1), F32),
-            pltpu.VMEM((2 * rows, units), F32),
-            pltpu.VMEM((2 * rows, units), F32),
+            pltpu.VMEM(theirs.shape, theirs.dtype),
+            pltpu.SemaphoreType.DMA((parts,)),
         ],
         cost_estimate=pl.CostEstimate(
             flops=8 * rows * width * units, bytes_accessed=1 << 22, transcendentals=1 << 16
         ),
-        compiler_params=pltpu.CompilerParams(
-            dimension_semantics=("arbitrary",), vmem_limit_bytes=8 << 20
-        ),
+        compiler_params=pltpu.CompilerParams(vmem_limit_bytes=8 << 20),
         name="hidden_units",
     )(mine, theirs, gain, gate, up)
 
@@ -157,11 +180,10 @@
     )(total)
 
 
-def mix_kernel(experts, cap, cols, tokens, route_pair, weight_pair, slots, mixed):
+def table_kernel(experts, cap, tokens, route_pair, weight_pair, table, widened):
     toks = tokens.shape[0]
     group = 2 * cap
-    keys = experts * group
-    row = lax.broadcasted_iota(jnp.int32, (keys, toks), 0)
+    row = lax.broadcasted_iota(jnp.int32, (experts * group, toks), 0)
     wanted = row // group
     pair = route_pair[...]
     weights = weight_pair[...]
@@ -171,12 +193,32 @@
     )
     share = jnp.where(picks, share, 0.0)
     side = lax.rem(row // cap, 2)
-    span = slots.shape[3]
+    for core in range(2):
+        table[core] = jnp.where(side == core, share, 0.0)
+    widened[...] = tokens[...].astype(F32)
+
+
+def mix_table(experts, cap, tokens, route_pair, weight_pair):
+    keys = experts * 2 * cap
+    return pl.pallas_call(
+        functools.partial(table_kernel, experts, cap),
+        out_shape=(
+            jax.ShapeDtypeStruct((2, keys, tokens.shape[0]), F32),
+            jax.ShapeDtypeStruct(tokens.shape, F32),
+        ),
+        cost_estimate=pl.CostEstimate(flops=1 << 18, bytes_accessed=1 << 18, transcendentals=0),
+        compiler_params=pltpu.CompilerParams(vmem_limit_bytes=8 << 20),
+        name="mix_table",
+    )(tokens, route_pair, weight_pair)
+
+
+def mix_kernel(cols, table, widened, slots, mixed):
+    keys, span = table.shape[1], slots.shape[3]
     for half in range(2):
         rows = slots[:, half].astype(F32).reshape(keys, span)
         parts = [
             lax.dot_general(
-                jnp.where(side == core, share, 0.0),
+                table[core],
                 rows,
                 (((0,), (0,)), ((), ())),
                 precision=lax.Precision.HIGHEST,
@@ -189,17 +231,17 @@
             cut = slice(block * cols, (block + 1) * cols)
             moe = jnp.concatenate([parts[0][:, cut], parts[1][:, cut]], axis=1)
             place = slice(base, base + 2 * cols)
-            mixed[:, place] = (tokens[:, place].astype(F32) + moe).astype(BF16)
-
-
-def mix_tokens(experts, cap, cols, tokens, route_pair, weight_pair, slots):
-    return pl.pallas_call(
-        functools.partial(mix_kernel, experts, cap, cols),
-        out_shape=jax.ShapeDtypeStruct(tokens.shape, BF16),
+            mixed[:, place] = (widened[:, place] + moe).astype(BF16)
+
+
+def mix_tokens(cols, table, widened, slots):
+    return pl.pallas_call(
+        functools.partial(mix_kernel, cols),
+        out_shape=jax.ShapeDtypeStruct(widened.shape, BF16),
         cost_estimate=pl.CostEstimate(flops=1 << 24, bytes_accessed=1 << 19, transcendentals=0),
         compiler_params=pltpu.CompilerParams(vmem_limit_bytes=8 << 20),
         name="mix_tokens",
-    )(tokens, route_pair, weight_pair, slots)
+    )(table, widened, slots)
 
 
 def layer(
@@ -240,10 +282,14 @@
     down = split_columns(down, n_xy)
     down = lax.all_to_all(down, XY, 0, 0, tiled=True).reshape(n_xy * cols, -1)
 
-    hid = hidden_units(experts, n_xy, mine, theirs, gain_sum, expert_gate[0], expert_up[0])
+    gate, up, _ = lax.optimization_barrier((expert_gate[0], expert_up[0], spread))
+    gate, up = stage(gate), stage(up)
+    hid = hidden_units(experts, n_xy, mine, theirs, gain_sum, gate, up)
     units = hid.shape[3]
     hid = hid.reshape(2 * n_xy * group, units)
     hid_far = lax.ppermute(hid, "zh", FLIP)
+    down = stage(down)
+    hid_far, down = lax.optimization_barrier((hid_far, down))
     near = jnp.concatenate(
         [jnp.where(half == 0, hid, hid_far), jnp.where(half == 0, hid_far, hid)], axis=1
     )
@@ -257,26 +303,35 @@
     ).astype(BF16)
     part = part.reshape(n_xy, 2 * group, n_xy * cols)
 
-    acc, _ = lax.optimization_barrier((keyval_weights[0], send))
-    until = dict(zip(steps, (hid, part, part)))
-    for step in steps:
+    def halve(acc, step):
         span = acc.shape[1] // 2
         upper = (expert // step) % 2 == 1
         stay = jnp.where(upper, acc[:, span:], acc[:, :span])
         leave = jnp.where(upper, acc[:, :span], acc[:, span:])
         came = lax.ppermute(leave, "branch", [(b, b ^ step) for b in range(experts)])
-        came, _ = lax.optimization_barrier((came, until[step]))
-        acc = stay.astype(F32) + came.astype(F32)
+        return stay, came
+
+    def join(stay, came, after):
+        came, _ = lax.optimization_barrier((came, after))
+        return stay.astype(F32) + came.astype(F32)
+
+    kv, _ = lax.optimization_barrier((keyval_weights[0], hid))
+    kv = join(*halve(kv, steps[0]), part)
+    kv = halve(kv, steps[1])
 
     part = lax.all_to_all(part, XY, 0, 0, tiled=True)
     total = jnp.sum(part.astype(F32), axis=0).astype(BF16)
+    kv = join(*kv, total)
     total = lax.all_gather(total, "core", axis=0, tiled=False)
     spread = fan_out(experts, cap, total)
+    kv, _ = lax.optimization_barrier((kv, spread))
+    kv = join(*halve(kv, steps[2]), spread)
     slots = lax.all_to_all(spread, ZLINE, 0, 0, tiled=True)
     slots = slots.reshape(experts, 2, group, n_xy * cols)
-    acc, _ = lax.optimization_barrier((acc, spread))
-    merged_keyval = (acc / experts).astype(BF16)
-    mixed = mix_tokens(experts, cap, cols, tokens, route_pair, weight_pair, slots)
+    late_tokens, _ = lax.optimization_barrier((tokens, spread))
+    merged_keyval = (kv / experts).astype(BF16)
+    table, widened = mix_table(experts, cap, late_tokens, route_pair, weight_pair)
+    mixed = mix_tokens(cols, table, widened, slots)
     return mixed, merged_keyval
 
 

time: 150 us -> 159 us (1.060)
  waiting for transfers between devices: 40.4 us -> 51.1 us
  starting transfers between devices: 67.4 us -> 70.4 us
    ppermute x3, waiting for transfers between devices: 9.6 us -> 33.4 us  [halve(): lax.ppermute(leave, 'branch', [(b, b ^ step) for b in range(experts)])]
    all_to_all x1, waiting for transfers between devices: 8.73 us -> 0.01 us  [layer(): slots = lax.all_to_all(spread, ZLINE, 0, 0, tiled=True)]
    all_to_all x1, waiting for transfers between devices: 6.84 us -> 0.01 us  [layer(): part = lax.all_to_all(part, XY, 0, 0, tiled=True)]
    ppermute x3, waiting for transfers between devices: 4.34 us -> 9.25 us  [layer(): lax.ppermute(gain_sum, 'branch', [(b, b ^ step) for b in range(experts)])]
    all_to_all x1, starting transfers between devices: 7.12 us -> 10.5 us  [layer(): slots = lax.all_to_all(spread, ZLINE, 0, 0, tiled=True)]
    ppermute x1, waiting for transfers between devices: 8.27 us -> 5.83 us  [layer(): hid_far = lax.ppermute(hid, 'zh', FLIP)]
    ppermute x1, starting transfers between devices: 7.89 us -> 10.2 us  [layer(): hid_far = lax.ppermute(hid, 'zh', FLIP)]
    ppermute x3, starting transfers between devices: 12.8 us -> 10.7 us  [halve(): lax.ppermute(leave, 'branch', [(b, b ^ step) for b in range(experts)])]
  transfers between devices with their start and end apart: 12 -> 12, of which waited for: 7 -> 8; matrix products, arithmetic and copies ran while one was open for 2% -> 1% of each run, Pallas kernels for 4% -> 2%
where the time goes in v5:
time: 159 us
  starting transfers between devices  70.4 us (44%)
  waiting for transfers between devices  51.1 us (32%)
  blocking collectives  24.9 us (16%)
  Pallas kernels  6.12 us (4%)
  local copies, waits for them, and re-layouts  2.78 us (2%)
    ppermute x3, waiting for transfers between devices, halve(): lax.ppermute(leave, 'branch', [(b, b ^ step) for b in range(experts)])  33.4 us
    all_to_all x1, blocking collectives, layer(): lax.all_to_all(spread, XY, 0, 0, tiled=True).reshape(n_xy * group, width)  21 us
    ppermute x1, starting transfers between devices, layer(): arrived = lax.ppermute(send, ZLINE, swap)  12.7 us
    ppermute x3, starting transfers between devices, layer(): lax.ppermute(gain_sum, 'branch', [(b, b ^ step) for b in range(experts)])  11.2 us
    ppermute x3, starting transfers between devices, halve(): lax.ppermute(leave, 'branch', [(b, b ^ step) for b in range(experts)])  10.7 us
    all_to_all x1, starting transfers between devices, layer(): slots = lax.all_to_all(spread, ZLINE, 0, 0, tiled=True)  10.5 us
    ppermute x1, starting transfers between devices, layer(): hid_far = lax.ppermute(hid, 'zh', FLIP)  10.2 us
    ppermute x3, waiting for transfers between devices, layer(): lax.ppermute(gain_sum, 'branch', [(b, b ^ step) for b in range(experts)])  9.25 us
  transfers between devices with their start and end apart: 12, of which 8 were waited for; matrix products, arithmetic and copies ran while one was open for 1% of the time, Pallas kernels for 2%

profile of v5, /device:TPU:6, one launch (start us, length us, event | category | flops | bytes accessed | tf_op | source)
XLA Modules:
  0.0 158.6 jit_solution(10543210074698744276)
XLA Ops:
  2.4 12.7 %collective-permute-start = (bf16[4,4096]{1,0:T(4,128)(2,1)S(1)}, bf16[4,4096]{1,0:T(4,128)(2,1)S(1)}, u32[]{:S(2)}, u32[]{:S(2)}) collective-permute-start(bf16[4,4096]{1,0:T(4,128)(2,1)S(1)} %get-tuple-element.19), channel_id=1, source_target_pairs={{0,258},{2,256},{64,322},{66,320},{128,386},{130,384},{192,450},{1... | collective-permute-start | bytes 98312 | tf_op jit(solution)/shard_map/ppermute | solution.py:266
  15.2 2.6 %collective-permute-done = bf16[4,4096]{1,0:T(4,128)(2,1)S(1)} collective-permute-done((bf16[4,4096]{1,0:T(4,128)(2,1)S(1)}, bf16[4,4096]{1,0:T(4,128)(2,1)S(1)}, u32[]{:S(2)}, u32[]{:S(2)}) %collective-permute-start) | collective-permute-done | bytes 32800 | tf_op jit(solution)/shard_map/ppermute | solution.py:266
  18.0 21.0 %all_to_all.20 = bf16[16,8,4096]{2,1,0:T(8,128)(2,1)S(1)} all-to-all(bf16[16,8,4096]{2,1,0:T(8,128)(2,1)S(1)} %broadcast_in_dim.2), channel_id=1, replica_groups=mesh['branch'=8,'x'=4,'y'=4,'zh'=2,'core'=2] {'x','y'}, dimensions={0} | all-to-all | bytes 2097152 | tf_op jit(solution)/shard_map/all_to_all | solution.py:270
  39.0 1.9 %collective-permute-start.1 = (bf16[128,4096]{1,0:T(8,128)(2,1)S(1)}, bf16[128,4096]{1,0:T(8,128)(2,1)}, u32[]{:S(2)}, u32[]{:S(2)}) collective-permute-start(bf16[128,4096]{1,0:T(8,128)(2,1)S(1)} %bitcast.27), channel_id=1, source_target_pairs={{0,1},{1,0},{2,3},{3,2},{4,5},{5,4},{6,7},{7,6},{8,9},{9,8},{10,11... | collective-permute-start | bytes 3145736 | tf_op jit(solution)/shard_map/ppermute | solution.py:271
  42.0 5.7 %all-to-all-start.1 = ((bf16[16,64,512]{2,1,0:T(8,128)(2,1)}), bf16[16,64,512]{2,1,0:T(8,128)(2,1)S(1)}, u32[]{:S(2)}, u32[]{:S(2)}) async-start(bf16[16,64,512]{2,1,0:T(8,128)(2,1)} %split_columns.1), calls=%async_computation.1 | async-start | bytes 2097152 | tf_op jit(solution)/shard_map/all_to_all | solution.py:283
  47.8 5.3 %collective-permute-start.2 = (f32[1,4096]{1,0:T(1,128)S(1)}, f32[1,4096]{1,0:T(1,128)S(1)}, u32[]{:S(2)}, u32[]{:S(2)}) collective-permute-start(f32[1,4096]{1,0:T(1,128)S(1)} %copy-done.8), channel_id=1, source_target_pairs={{0,256},{64,320},{128,384},{192,448},{256,0},{320,64},{384,128},{4... | collective-permute-start | bytes 49160 | tf_op jit(solution)/shard_map/ppermute | solution.py:275
  53.1 4.4 %collective-permute-done.2 = f32[1,4096]{1,0:T(1,128)S(1)} collective-permute-done((f32[1,4096]{1,0:T(1,128)S(1)}, f32[1,4096]{1,0:T(1,128)S(1)}, u32[]{:S(2)}, u32[]{:S(2)}) %collective-permute-start.2) | collective-permute-done | bytes 16416 | tf_op jit(solution)/shard_map/ppermute | solution.py:275
  57.5 3.1 %collective-permute-start.3 = (f32[1,4096]{1,0:T(1,128)S(1)}, f32[1,4096]{1,0:T(1,128)S(1)}, u32[]{:S(2)}, u32[]{:S(2)}) collective-permute-start(f32[1,4096]{1,0:T(1,128)S(1)} %add.33), channel_id=1, source_target_pairs={{0,128},{64,192},{128,0},{192,64},{256,384},{320,448},{384,256},{4... | collective-permute-start | bytes 49160 | tf_op jit(solution)/shard_map/ppermute | solution.py:275
  60.6 3.5 %collective-permute-done.3 = f32[1,4096]{1,0:T(1,128)S(1)} collective-permute-done((f32[1,4096]{1,0:T(1,128)S(1)}, f32[1,4096]{1,0:T(1,128)S(1)}, u32[]{:S(2)}, u32[]{:S(2)}) %collective-permute-start.3) | collective-permute-done | bytes 16416 | tf_op jit(solution)/shard_map/ppermute | solution.py:275
  64.1 2.9 %collective-permute-start.4 = (f32[1,4096]{1,0:T(1,128)S(1)}, f32[1,4096]{1,0:T(1,128)S(1)}, u32[]{:S(2)}, u32[]{:S(2)}) collective-permute-start(f32[1,4096]{1,0:T(1,128)S(1)} %add.34), channel_id=1, source_target_pairs={{0,64},{64,0},{128,192},{192,128},{256,320},{320,256},{384,448},{4... | collective-permute-start | bytes 49160 | tf_op jit(solution)/shard_map/ppermute | solution.py:275
  68.3 1.4 collective-permute-done.4
  69.7 2.3 %hidden_units.1 = bf16[16,2,8,128]{3,2,1,0:T(8,128)(2,1)S(1)} custom-call(bf16[128,4096]{1,0:T(8,128)(2,1)S(1)} %bitcast.28, bf16[128,4096]{1,0:T(8,128)(2,1)} %collective-permute-done.1.theirs_hbm, f32[1,4096]{1,0:T(1,128)S(1)} %add.35.gain, bf16[4096,128]{1,0:T(8,128)(2,1)S(1)} %stage.3.gate, bf16[4096,128]{1,0:T(8,128)(2,1)S(1)} %stage.4.up), custom_call_target="tpu_custom_call" | custom-call | flops 536870912 | bytes 4194304 | tf_op jit(solution)/shard_map/hidden_units/pallas_call | solution.py:142
  72.0 10.2 %collective-permute-start.5 = (bf16[256,128]{1,0:T(8,128)(2,1)S(1)}, bf16[256,128]{1,0:T(8,128)(2,1)S(1)}, u32[]{:S(2)}, u32[]{:S(2)}) collective-permute-start(bf16[256,128]{1,0:T(8,128)(2,1)S(1)} %bitcast.33), channel_id=1, source_target_pairs={{0,2},{2,0},{1,3},{3,1},{4,6},{6,4},{5,7},{7,5},{8,10},{10,8},{9,1... | collective-permute-start | bytes 196616 | tf_op jit(solution)/shard_map/ppermute | solution.py:290
  82.4 5.8 %collective-permute-done.5 = bf16[256,128]{1,0:T(8,128)(2,1)S(1)} collective-permute-done((bf16[256,128]{1,0:T(8,128)(2,1)S(1)}, bf16[256,128]{1,0:T(8,128)(2,1)S(1)}, u32[]{:S(2)}, u32[]{:S(2)}) %collective-permute-start.5) | collective-permute-done | bytes 65568 | tf_op jit(solution)/shard_map/ppermute | solution.py:290
  88.3 2.0 %all-gather = bf16[512,256]{1,0:T(8,128)(2,1)S(1)} all-gather(bf16[256,256]{1,0:T(8,128)(2,1)S(1)} %pad_maximum_fusion), channel_id=2, replica_groups=mesh['branch'=8,'x'=4,'y'=4,'zh'=2,'core'=2] {'core'}, dimensions={0}, use_global_device_ids=true | all-gather | bytes 393216 | tf_op jit(solution)/shard_map/all_gather | solution.py:296
  91.6 7.3 %all-to-all-start.2 = ((bf16[16,16,1024]{2,1,0:T(8,128)(2,1)}), bf16[16,16,1024]{2,1,0:T(8,128)(2,1)S(1)}, u32[]{:S(2)}, u32[]{:S(2)}) async-start(bf16[16,16,1024]{2,1,0:T(8,128)(2,1)} %bitcast.13), calls=%async_computation.2 | async-start | bytes 1048576 | tf_op jit(solution)/shard_map/all_to_all | solution.py:322
  99.0 4.0 %collective-permute-start.6 = (bf16[64,1024]{1,0:T(8,128)(2,1)S(1)}, bf16[64,1024]{1,0:T(8,128)(2,1)S(1)}, u32[]{:S(2)}, u32[]{:S(2)}) collective-permute-start(bf16[64,1024]{1,0:T(8,128)(2,1)S(1)} %broadcast_select_fusion), channel_id=1, source_target_pairs={{0,256},{64,320},{128,384},{192,448},{256,0},{320,64},{384,128},{4... | collective-permute-start | bytes 393224 | tf_op jit(solution)/shard_map/ppermute | solution.py:311
  103.0 14.3 %collective-permute-done.6 = bf16[64,1024]{1,0:T(8,128)(2,1)S(1)} collective-permute-done((bf16[64,1024]{1,0:T(8,128)(2,1)S(1)}, bf16[64,1024]{1,0:T(8,128)(2,1)S(1)}, u32[]{:S(2)}, u32[]{:S(2)}) %collective-permute-start.6) | collective-permute-done | bytes 131104 | tf_op jit(solution)/shard_map/ppermute | solution.py:311
  117.5 1.9 %all-gather.1 = bf16[32,1024]{1,0:T(8,128)(2,1)S(1)} all-gather(bf16[16,1024]{1,0:T(8,128)(2,1)S(1)} %reduce_sum.12), channel_id=3, replica_groups=mesh['branch'=8,'x'=4,'y'=4,'zh'=2,'core'=2] {'core'}, dimensions={0}, use_global_device_ids=true | all-gather | bytes 98304 | tf_op jit(solution)/shard_map/all_gather | solution.py:325
  120.1 10.5 %all-to-all-start.3 = ((bf16[16,8,1024]{2,1,0:T(8,128)(2,1)}), bf16[16,8,1024]{2,1,0:T(8,128)(2,1)S(1)}, u32[]{:S(2)}, u32[]{:S(2)}) async-start(bf16[16,8,1024]{2,1,0:T(8,128)(2,1)} %fan_out.1), calls=%async_computation.3 | async-start | bytes 524288 | tf_op jit(solution)/shard_map/all_to_all | solution.py:329
  130.6 4.7 %collective-permute-start.7 = (f32[64,512]{1,0:T(8,128)S(1)}, f32[64,512]{1,0:T(8,128)S(1)}, u32[]{:S(2)}, u32[]{:S(2)}) collective-permute-start(f32[64,512]{1,0:T(8,128)S(1)} %slice_select_fusion), channel_id=1, source_target_pairs={{0,128},{64,192},{128,0},{192,64},{256,384},{320,448},{384,256},{4... | collective-permute-start | bytes 393224 | tf_op jit(solution)/shard_map/ppermute | solution.py:311
  135.4 15.1 %collective-permute-done.7 = f32[64,512]{1,0:T(8,128)S(1)} collective-permute-done((f32[64,512]{1,0:T(8,128)S(1)}, f32[64,512]{1,0:T(8,128)S(1)}, u32[]{:S(2)}, u32[]{:S(2)}) %collective-permute-start.7) | collective-permute-done | bytes 131104 | tf_op jit(solution)/shard_map/ppermute | solution.py:311
  150.5 1.9 %collective-permute-start.8 = (f32[64,256]{1,0:T(8,128)S(1)}, f32[64,256]{1,0:T(8,128)S(1)}, u32[]{:S(2)}, u32[]{:S(2)}) collective-permute-start(f32[64,256]{1,0:T(8,128)S(1)} %slice_select_fusion.1), channel_id=1, source_target_pairs={{0,64},{64,0},{128,192},{192,128},{256,320},{320,256},{384,448},{4... | collective-permute-start | bytes 196616 | tf_op jit(solution)/shard_map/ppermute | solution.py:311
  152.6 4.1 %collective-permute-done.8 = f32[64,256]{1,0:T(8,128)S(1)} collective-permute-done((f32[64,256]{1,0:T(8,128)S(1)}, f32[64,256]{1,0:T(8,128)S(1)}, u32[]{:S(2)}, u32[]{:S(2)}) %collective-permute-start.8) | collective-permute-done | bytes 65568 | tf_op jit(solution)/shard_map/ppermute | solution.py:311
  (48 shorter events, 8.9 us)
Async XLA Ops:
  0.6 0.7 copy-start.5
  1.3 0.8 copy-start.3
  2.4 15.4 %collective-permute-start = (bf16[4,4096]{1,0:T(4,128)(2,1)S(1)}, bf16[4,4096]{1,0:T(4,128)(2,1)S(1)}, u32[]{:S(2)}, u32[]{:S(2)}) collective-permute-start(bf16[4,4096]{1,0:T(4,128)(2,1)S(1)} %get-tuple-element.19), channel_id=1, source_target_pairs={{0,258},{2,256},{64,322},{66,320},{128,386},{130,384},{192,450},{1... | collective-permute-start | bytes 98312 | tf_op jit(solution)/shard_map/ppermute | solution.py:266
  18.0 22.9 %copy-start = (bf16[1,8192,64]{1,2,0:T(8,128)(2,1)S(1)}, bf16[1,8192,64]{1,2,0:T(8,128)(2,1)}, u32[]{:S(2)}) copy-start(bf16[1,8192,64]{1,2,0:T(8,128)(2,1)} %param.15) | copy-start | bytes 3145732
  39.0 30.7 %collective-permute-start.1 = (bf16[128,4096]{1,0:T(8,128)(2,1)S(1)}, bf16[128,4096]{1,0:T(8,128)(2,1)}, u32[]{:S(2)}, u32[]{:S(2)}) collective-permute-start(bf16[128,4096]{1,0:T(8,128)(2,1)S(1)} %bitcast.27), channel_id=1, source_target_pairs={{0,1},{1,0},{2,3},{3,2},{4,5},{5,4},{6,7},{7,6},{8,9},{9,8},{10,11... | collective-permute-start | bytes 3145736 | tf_op jit(solution)/shard_map/ppermute | solution.py:271
  42.0 5.7 %copy-start.8 = (f32[1,4096]{1,0:T(1,128)S(1)}, f32[1,4096]{1,0:T(1,128)}, u32[]{:S(2)}) copy-start(f32[1,4096]{1,0:T(1,128)} %param.11) | copy-start | bytes 49156
  42.0 24.9 %copy-start.1 = (bf16[1,4096,128]{2,1,0:T(8,128)(2,1)S(1)}, bf16[1,4096,128]{2,1,0:T(8,128)(2,1)}, u32[]{:S(2)}) copy-start(bf16[1,4096,128]{2,1,0:T(8,128)(2,1)} %param.13) | copy-start | bytes 3145732
  42.0 40.2 %all-to-all-start.1 = ((bf16[16,64,512]{2,1,0:T(8,128)(2,1)}), bf16[16,64,512]{2,1,0:T(8,128)(2,1)S(1)}, u32[]{:S(2)}, u32[]{:S(2)}) async-start(bf16[16,64,512]{2,1,0:T(8,128)(2,1)} %split_columns.1), calls=%async_computation.1 | async-start | bytes 2097152 | tf_op jit(solution)/shard_map/all_to_all | solution.py:283
  47.8 9.7 %collective-permute-start.2 = (f32[1,4096]{1,0:T(1,128)S(1)}, f32[1,4096]{1,0:T(1,128)S(1)}, u32[]{:S(2)}, u32[]{:S(2)}) collective-permute-start(f32[1,4096]{1,0:T(1,128)S(1)} %copy-done.8), channel_id=1, source_target_pairs={{0,256},{64,320},{128,384},{192,448},{256,0},{320,64},{384,128},{4... | collective-permute-start | bytes 49160 | tf_op jit(solution)/shard_map/ppermute | solution.py:275
  57.5 6.5 %collective-permute-start.3 = (f32[1,4096]{1,0:T(1,128)S(1)}, f32[1,4096]{1,0:T(1,128)S(1)}, u32[]{:S(2)}, u32[]{:S(2)}) collective-permute-start(f32[1,4096]{1,0:T(1,128)S(1)} %add.33), channel_id=1, source_target_pairs={{0,128},{64,192},{128,0},{192,64},{256,384},{320,448},{384,256},{4... | collective-permute-start | bytes 49160 | tf_op jit(solution)/shard_map/ppermute | solution.py:275
  64.1 5.6 %collective-permute-start.4 = (f32[1,4096]{1,0:T(1,128)S(1)}, f32[1,4096]{1,0:T(1,128)S(1)}, u32[]{:S(2)}, u32[]{:S(2)}) collective-permute-start(f32[1,4096]{1,0:T(1,128)S(1)} %add.34), channel_id=1, source_target_pairs={{0,64},{64,0},{128,192},{192,128},{256,320},{320,256},{384,448},{4... | collective-permute-start | bytes 49160 | tf_op jit(solution)/shard_map/ppermute | solution.py:275
  67.0 1.2 copy-start.2
  72.0 16.2 %collective-permute-start.5 = (bf16[256,128]{1,0:T(8,128)(2,1)S(1)}, bf16[256,128]{1,0:T(8,128)(2,1)S(1)}, u32[]{:S(2)}, u32[]{:S(2)}) collective-permute-start(bf16[256,128]{1,0:T(8,128)(2,1)S(1)} %bitcast.33), channel_id=1, source_target_pairs={{0,2},{2,0},{1,3},{3,1},{4,6},{6,4},{5,7},{7,5},{8,10},{10,8},{9,1... | collective-permute-start | bytes 196616 | tf_op jit(solution)/shard_map/ppermute | solution.py:290
  91.6 7.3 %copy-start.7 = (bf16[1,64,2048]{2,1,0:T(8,128)(2,1)S(1)}, bf16[1,64,2048]{2,1,0:T(8,128)(2,1)}, u32[]{:S(2)}) copy-start(bf16[1,64,2048]{2,1,0:T(8,128)(2,1)} %param.12) | copy-start | bytes 786436
  91.6 25.8 %all-to-all-start.2 = ((bf16[16,16,1024]{2,1,0:T(8,128)(2,1)}), bf16[16,16,1024]{2,1,0:T(8,128)(2,1)S(1)}, u32[]{:S(2)}, u32[]{:S(2)}) async-start(bf16[16,16,1024]{2,1,0:T(8,128)(2,1)} %bitcast.13), calls=%async_computation.2 | async-start | bytes 1048576 | tf_op jit(solution)/shard_map/all_to_all | solution.py:322
  99.0 18.4 %collective-permute-start.6 = (bf16[64,1024]{1,0:T(8,128)(2,1)S(1)}, bf16[64,1024]{1,0:T(8,128)(2,1)S(1)}, u32[]{:S(2)}, u32[]{:S(2)}) collective-permute-start(bf16[64,1024]{1,0:T(8,128)(2,1)S(1)} %broadcast_select_fusion), channel_id=1, source_target_pairs={{0,256},{64,320},{128,384},{192,448},{256,0},{320,64},{384,128},{4... | collective-permute-start | bytes 393224 | tf_op jit(solution)/shard_map/ppermute | solution.py:311
  120.1 37.2 %all-to-all-start.3 = ((bf16[16,8,1024]{2,1,0:T(8,128)(2,1)}), bf16[16,8,1024]{2,1,0:T(8,128)(2,1)S(1)}, u32[]{:S(2)}, u32[]{:S(2)}) async-start(bf16[16,8,1024]{2,1,0:T(8,128)(2,1)} %fan_out.1), calls=%async_computation.3 | async-start | bytes 524288 | tf_op jit(solution)/shard_map/all_to_all | solution.py:329
  130.6 19.8 %collective-permute-start.7 = (f32[64,512]{1,0:T(8,128)S(1)}, f32[64,512]{1,0:T(8,128)S(1)}, u32[]{:S(2)}, u32[]{:S(2)}) collective-permute-start(f32[64,512]{1,0:T(8,128)S(1)} %slice_select_fusion), channel_id=1, source_target_pairs={{0,128},{64,192},{128,0},{192,64},{256,384},{320,448},{384,256},{4... | collective-permute-start | bytes 393224 | tf_op jit(solution)/shard_map/ppermute | solution.py:311
  150.4 2.0 %copy-start.4 = (bf16[8,4096]{1,0:T(8,128)(2,1)S(1)}, bf16[8,4096]{1,0:T(8,128)(2,1)}, u32[]{:S(2)}) copy-start(bf16[8,4096]{1,0:T(8,128)(2,1)} %tokens.2) | copy-start | bytes 196612
  150.5 2.0 %copy-start.6 = (f32[8,2]{0,1:T(2,128)S(1)}, f32[8,2]{0,1:T(2,128)}, u32[]{:S(2)}) copy-start(f32[8,2]{0,1:T(2,128)} %param.10) | copy-start | bytes 196
  150.5 6.2 %collective-permute-start.8 = (f32[64,256]{1,0:T(8,128)S(1)}, f32[64,256]{1,0:T(8,128)S(1)}, u32[]{:S(2)}, u32[]{:S(2)}) collective-permute-start(f32[64,256]{1,0:T(8,128)S(1)} %slice_select_fusion.1), channel_id=1, source_target_pairs={{0,64},{64,0},{128,192},{192,128},{256,320},{320,256},{384,448},{4... | collective-permute-start | bytes 196616 | tf_op jit(solution)/shard_map/ppermute | solution.py:311

commit v6 on v5

--- a/solution.py
+++ b/solution.py
@@ -193,8 +193,14 @@
     )
     share = jnp.where(picks, share, 0.0)
     side = lax.rem(row // cap, 2)
+    terms = []
     for core in range(2):
-        table[core] = jnp.where(side == core, share, 0.0)
+        rest = jnp.where(side == core, share, 0.0)
+        for _ in range(3):
+            term = rest.astype(BF16)
+            rest = rest - term.astype(F32)
+            terms.append(term.astype(F32))
+    table[...] = jnp.concatenate(terms, axis=1).astype(BF16)
     widened[...] = tokens[...].astype(F32)
 
 
@@ -203,7 +209,7 @@
     return pl.pallas_call(
         functools.partial(table_kernel, experts, cap),
         out_shape=(
-            jax.ShapeDtypeStruct((2, keys, tokens.shape[0]), F32),
+            jax.ShapeDtypeStruct((keys, 6 * tokens.shape[0]), BF16),
             jax.ShapeDtypeStruct(tokens.shape, F32),
         ),
         cost_estimate=pl.CostEstimate(flops=1 << 18, bytes_accessed=1 << 18, transcendentals=0),
@@ -213,19 +219,15 @@
 
 
 def mix_kernel(cols, table, widened, slots, mixed):
-    keys, span = table.shape[1], slots.shape[3]
+    keys, span = table.shape[0], slots.shape[3]
+    toks = widened.shape[0]
     for half in range(2):
-        rows = slots[:, half].astype(F32).reshape(keys, span)
-        parts = [
-            lax.dot_general(
-                table[core],
-                rows,
-                (((0,), (0,)), ((), ())),
-                precision=lax.Precision.HIGHEST,
-                preferred_element_type=F32,
-            )
-            for core in range(2)
-        ]
+        rows = slots[:, half].reshape(keys, span)
+        sums = lax.dot_general(
+            table[...], rows, (((0,), (0,)), ((), ())), preferred_element_type=F32
+        )
+        terms = [sums[toks * term : toks * (term + 1)] for term in range(6)]
+        parts = [terms[3 * core] + terms[3 * core + 1] + terms[3 * core + 2] for core in range(2)]
         for block in range(span // cols):
             base = (block * 4 + half * 2) * cols
             cut = slice(block * cols, (block + 1) * cols)
@@ -271,9 +273,9 @@
     theirs = lax.ppermute(mine, "core", FLIP)
 
     gain_sum = norm_gains
-    for step in steps:
+    for step in reversed(steps):
         came = lax.ppermute(gain_sum, "branch", [(b, b ^ step) for b in range(experts)])
-        if step == steps[0]:
+        if step == steps[-1]:
             came, _ = lax.optimization_barrier((came, spread))
         gain_sum = gain_sum + came
 
@@ -303,11 +305,17 @@
     ).astype(BF16)
     part = part.reshape(n_xy, 2 * group, n_xy * cols)
 
+    kv_cols = keyval_weights.shape[2] // experts
+
     def halve(acc, step):
-        span = acc.shape[1] // 2
+        blocks = jnp.split(acc, acc.shape[1] // kv_cols, axis=1)
+        even = jnp.concatenate(blocks[0::2], axis=1)
+        odd = jnp.concatenate(blocks[1::2], axis=1)
         upper = (expert // step) % 2 == 1
-        stay = jnp.where(upper, acc[:, span:], acc[:, :span])
-        leave = jnp.where(upper, acc[:, :span], acc[:, span:])
+        stay = jnp.where(upper, odd, even)
+        leave = jnp.where(upper, even, odd)
+        if len(blocks) == 2:
+            leave = leave.astype(BF16)
         came = lax.ppermute(leave, "branch", [(b, b ^ step) for b in range(experts)])
         return stay, came
 
@@ -316,7 +324,7 @@
         return stay.astype(F32) + came.astype(F32)
 
     kv, _ = lax.optimization_barrier((keyval_weights[0], hid))
-    kv = join(*halve(kv, steps[0]), part)
+    kv = join(*halve(kv, steps[2]), part)
     kv = halve(kv, steps[1])
 
     part = lax.all_to_all(part, XY, 0, 0, tiled=True)
@@ -325,7 +333,7 @@
     total = lax.all_gather(total, "core", axis=0, tiled=False)
     spread = fan_out(experts, cap, total)
     kv, _ = lax.optimization_barrier((kv, spread))
-    kv = join(*halve(kv, steps[2]), spread)
+    kv = join(*halve(kv, steps[0]), spread)
     slots = lax.all_to_all(spread, ZLINE, 0, 0, tiled=True)
     slots = slots.reshape(experts, 2, group, n_xy * cols)
     late_tokens, _ = lax.optimization_barrier((tokens, spread))

time: 159 us -> 154 us (0.969)
  waiting for transfers between devices: 51.1 us -> 42 us
  starting transfers between devices: 70.4 us -> 73.7 us
    ppermute x3, waiting for transfers between devices: 33.4 us -> 22 us  [halve(): lax.ppermute(leave, 'branch', [(b, b ^ step) for b in range(experts)])]
    ppermute x3, starting transfers between devices: 10.7 us -> 14.4 us  [halve(): lax.ppermute(leave, 'branch', [(b, b ^ step) for b in range(experts)])]
    all_to_all x1, waiting for transfers between devices: 0.01 us -> 2.76 us  [layer(): part = lax.all_to_all(part, XY, 0, 0, tiled=True)]
  transfers between devices with their start and end apart: 12 -> 12, of which waited for: 8 -> 9; matrix products, arithmetic and copies ran while one was open for 1% -> 1% of each run, Pallas kernels for 2% -> 3%
where the time goes in v6:
time: 154 us; the launch traced here: 153 us
  starting transfers between devices  73.7 us (48%)
  waiting for transfers between devices  42 us (27%)
  blocking collectives  24.9 us (16%)
  Pallas kernels  5.87 us (4%)
  local copies, waits for them, and re-layouts  2.82 us (2%)
    ppermute x3, waiting for transfers between devices, halve(): lax.ppermute(leave, 'branch', [(b, b ^ step) for b in range(experts)])  22 us
    all_to_all x1, blocking collectives, layer(): lax.all_to_all(spread, XY, 0, 0, tiled=True).reshape(n_xy * group, width)  21 us
    ppermute x3, starting transfers between devices, halve(): lax.ppermute(leave, 'branch', [(b, b ^ step) for b in range(experts)])  14.4 us
    ppermute x1, starting transfers between devices, layer(): arrived = lax.ppermute(send, ZLINE, swap)  12.7 us
    ppermute x3, starting transfers between devices, layer(): lax.ppermute(gain_sum, 'branch', [(b, b ^ step) for b in range(experts)])  11.4 us
    ppermute x1, starting transfers between devices, layer(): hid_far = lax.ppermute(hid, 'zh', FLIP)  10.4 us
    all_to_all x1, starting transfers between devices, layer(): slots = lax.all_to_all(spread, ZLINE, 0, 0, tiled=True)  9.77 us
    ppermute x3, waiting for transfers between devices, layer(): lax.ppermute(gain_sum, 'branch', [(b, b ^ step) for b in range(experts)])  8.9 us
  transfers between devices with their start and end apart: 12, of which 9 were waited for; matrix products, arithmetic and copies ran while one was open for 1% of the time, Pallas kernels for 3%

profile of v6, /device:TPU:6, one launch (start us, length us, event | category | flops | bytes accessed | tf_op | source)
XLA Modules:
  0.0 152.6 jit_solution(18303918980554497322)
XLA Ops:
  2.4 12.7 %collective-permute-start = (bf16[4,4096]{1,0:T(4,128)(2,1)S(1)}, bf16[4,4096]{1,0:T(4,128)(2,1)S(1)}, u32[]{:S(2)}, u32[]{:S(2)}) collective-permute-start(bf16[4,4096]{1,0:T(4,128)(2,1)S(1)} %get-tuple-element.19), channel_id=1, source_target_pairs={{0,258},{2,256},{64,322},{66,320},{128,386},{130,384},{192,450},{1... | collective-permute-start | bytes 98312 | tf_op jit(solution)/shard_map/ppermute | solution.py:268
  15.2 2.6 %collective-permute-done = bf16[4,4096]{1,0:T(4,128)(2,1)S(1)} collective-permute-done((bf16[4,4096]{1,0:T(4,128)(2,1)S(1)}, bf16[4,4096]{1,0:T(4,128)(2,1)S(1)}, u32[]{:S(2)}, u32[]{:S(2)}) %collective-permute-start) | collective-permute-done | bytes 32800 | tf_op jit(solution)/shard_map/ppermute | solution.py:268
  18.0 21.0 %all_to_all.20 = bf16[16,8,4096]{2,1,0:T(8,128)(2,1)S(1)} all-to-all(bf16[16,8,4096]{2,1,0:T(8,128)(2,1)S(1)} %broadcast_in_dim.2), channel_id=1, replica_groups=mesh['branch'=8,'x'=4,'y'=4,'zh'=2,'core'=2] {'x','y'}, dimensions={0} | all-to-all | bytes 2097152 | tf_op jit(solution)/shard_map/all_to_all | solution.py:272
  39.0 1.9 %collective-permute-start.1 = (bf16[128,4096]{1,0:T(8,128)(2,1)S(1)}, bf16[128,4096]{1,0:T(8,128)(2,1)}, u32[]{:S(2)}, u32[]{:S(2)}) collective-permute-start(bf16[128,4096]{1,0:T(8,128)(2,1)S(1)} %bitcast.27), channel_id=1, source_target_pairs={{0,1},{1,0},{2,3},{3,2},{4,5},{5,4},{6,7},{7,6},{8,9},{9,8},{10,11... | collective-permute-start | bytes 3145736 | tf_op jit(solution)/shard_map/ppermute | solution.py:273
  42.0 5.7 %all-to-all-start.1 = ((bf16[16,64,512]{2,1,0:T(8,128)(2,1)}), bf16[16,64,512]{2,1,0:T(8,128)(2,1)S(1)}, u32[]{:S(2)}, u32[]{:S(2)}) async-start(bf16[16,64,512]{2,1,0:T(8,128)(2,1)} %split_columns.1), calls=%async_computation.1 | async-start | bytes 2097152 | tf_op jit(solution)/shard_map/all_to_all | solution.py:285
  47.8 2.9 %collective-permute-start.2 = (f32[1,4096]{1,0:T(1,128)S(1)}, f32[1,4096]{1,0:T(1,128)S(1)}, u32[]{:S(2)}, u32[]{:S(2)}) collective-permute-start(f32[1,4096]{1,0:T(1,128)S(1)} %copy-done.8), channel_id=1, source_target_pairs={{0,64},{64,0},{128,192},{192,128},{256,320},{320,256},{384,448},{4... | collective-permute-start | bytes 49160 | tf_op jit(solution)/shard_map/ppermute | solution.py:277
  50.6 2.7 %collective-permute-done.2 = f32[1,4096]{1,0:T(1,128)S(1)} collective-permute-done((f32[1,4096]{1,0:T(1,128)S(1)}, f32[1,4096]{1,0:T(1,128)S(1)}, u32[]{:S(2)}, u32[]{:S(2)}) %collective-permute-start.2) | collective-permute-done | bytes 16416 | tf_op jit(solution)/shard_map/ppermute | solution.py:277
  53.4 3.2 %collective-permute-start.3 = (f32[1,4096]{1,0:T(1,128)S(1)}, f32[1,4096]{1,0:T(1,128)S(1)}, u32[]{:S(2)}, u32[]{:S(2)}) collective-permute-start(f32[1,4096]{1,0:T(1,128)S(1)} %add.33), channel_id=1, source_target_pairs={{0,128},{64,192},{128,0},{192,64},{256,384},{320,448},{384,256},{4... | collective-permute-start | bytes 49160 | tf_op jit(solution)/shard_map/ppermute | solution.py:277
  56.7 3.3 %collective-permute-done.3 = f32[1,4096]{1,0:T(1,128)S(1)} collective-permute-done((f32[1,4096]{1,0:T(1,128)S(1)}, f32[1,4096]{1,0:T(1,128)S(1)}, u32[]{:S(2)}, u32[]{:S(2)}) %collective-permute-start.3) | collective-permute-done | bytes 16416 | tf_op jit(solution)/shard_map/ppermute | solution.py:277
  60.0 5.3 %collective-permute-start.4 = (f32[1,4096]{1,0:T(1,128)S(1)}, f32[1,4096]{1,0:T(1,128)S(1)}, u32[]{:S(2)}, u32[]{:S(2)}) collective-permute-start(f32[1,4096]{1,0:T(1,128)S(1)} %add.34), channel_id=1, source_target_pairs={{0,256},{64,320},{128,384},{192,448},{256,0},{320,64},{384,128},{4... | collective-permute-start | bytes 49160 | tf_op jit(solution)/shard_map/ppermute | solution.py:277
  66.6 2.9 %collective-permute-done.4 = f32[1,4096]{1,0:T(1,128)S(1)} collective-permute-done((f32[1,4096]{1,0:T(1,128)S(1)}, f32[1,4096]{1,0:T(1,128)S(1)}, u32[]{:S(2)}, u32[]{:S(2)}) %collective-permute-start.4) | collective-permute-done | bytes 16416 | tf_op jit(solution)/shard_map/ppermute | solution.py:277
  69.5 2.3 %hidden_units.1 = bf16[16,2,8,128]{3,2,1,0:T(8,128)(2,1)S(1)} custom-call(bf16[128,4096]{1,0:T(8,128)(2,1)S(1)} %bitcast.28, bf16[128,4096]{1,0:T(8,128)(2,1)} %collective-permute-done.1.theirs_hbm, f32[1,4096]{1,0:T(1,128)S(1)} %add.35.gain, bf16[4096,128]{1,0:T(8,128)(2,1)S(1)} %stage.3.gate, bf16[4096,128]{1,0:T(8,128)(2,1)S(1)} %stage.4.up), custom_call_target="tpu_custom_call" | custom-call | flops 536870912 | bytes 4194304 | tf_op jit(solution)/shard_map/hidden_units/pallas_call | solution.py:142
  71.8 10.4 %collective-permute-start.5 = (bf16[256,128]{1,0:T(8,128)(2,1)S(1)}, bf16[256,128]{1,0:T(8,128)(2,1)S(1)}, u32[]{:S(2)}, u32[]{:S(2)}) collective-permute-start(bf16[256,128]{1,0:T(8,128)(2,1)S(1)} %bitcast.33), channel_id=1, source_target_pairs={{0,2},{2,0},{1,3},{3,1},{4,6},{6,4},{5,7},{7,5},{8,10},{10,8},{9,1... | collective-permute-start | bytes 196616 | tf_op jit(solution)/shard_map/ppermute | solution.py:292
  82.4 5.7 %collective-permute-done.5 = bf16[256,128]{1,0:T(8,128)(2,1)S(1)} collective-permute-done((bf16[256,128]{1,0:T(8,128)(2,1)S(1)}, bf16[256,128]{1,0:T(8,128)(2,1)S(1)}, u32[]{:S(2)}, u32[]{:S(2)}) %collective-permute-start.5) | collective-permute-done | bytes 65568 | tf_op jit(solution)/shard_map/ppermute | solution.py:292
  88.1 2.0 %all-gather = bf16[512,256]{1,0:T(8,128)(2,1)S(1)} all-gather(bf16[256,256]{1,0:T(8,128)(2,1)S(1)} %pad_maximum_fusion), channel_id=2, replica_groups=mesh['branch'=8,'x'=4,'y'=4,'zh'=2,'core'=2] {'core'}, dimensions={0}, use_global_device_ids=true | all-gather | bytes 393216 | tf_op jit(solution)/shard_map/all_gather | solution.py:298
  91.5 7.3 %all-to-all-start.2 = ((bf16[16,16,1024]{2,1,0:T(8,128)(2,1)}), bf16[16,16,1024]{2,1,0:T(8,128)(2,1)S(1)}, u32[]{:S(2)}, u32[]{:S(2)}) async-start(bf16[16,16,1024]{2,1,0:T(8,128)(2,1)} %bitcast.13), calls=%async_computation.2 | async-start | bytes 1048576 | tf_op jit(solution)/shard_map/all_to_all | solution.py:330
  98.9 1.9 %collective-permute-start.6 = (bf16[64,1024]{1,0:T(8,128)(2,1)S(1)}, bf16[64,1024]{1,0:T(8,128)(2,1)S(1)}, u32[]{:S(2)}, u32[]{:S(2)}) collective-permute-start(bf16[64,1024]{1,0:T(8,128)(2,1)S(1)} %broadcast_select_fusion), channel_id=1, source_target_pairs={{0,64},{64,0},{128,192},{192,128},{256,320},{320,256},{384,448},{4... | collective-permute-start | bytes 393224 | tf_op jit(solution)/shard_map/ppermute | solution.py:319
  100.8 4.9 %collective-permute-done.6 = bf16[64,1024]{1,0:T(8,128)(2,1)S(1)} collective-permute-done((bf16[64,1024]{1,0:T(8,128)(2,1)S(1)}, bf16[64,1024]{1,0:T(8,128)(2,1)S(1)}, u32[]{:S(2)}, u32[]{:S(2)}) %collective-permute-start.6) | collective-permute-done | bytes 131104 | tf_op jit(solution)/shard_map/ppermute | solution.py:319
  105.8 2.8 %all-to-all-done.2 = bf16[16,16,1024]{2,1,0:T(8,128)(2,1)S(1)} async-done(((bf16[16,16,1024]{2,1,0:T(8,128)(2,1)}), bf16[16,16,1024]{2,1,0:T(8,128)(2,1)S(1)}, u32[]{:S(2)}, u32[]{:S(2)}) %all-to-all-start.2) | async-done | bytes 524320 | tf_op jit(solution)/shard_map/all_to_all | solution.py:330
  111.2 9.8 %all-to-all-start.3 = ((bf16[16,8,1024]{2,1,0:T(8,128)(2,1)}), bf16[16,8,1024]{2,1,0:T(8,128)(2,1)S(1)}, u32[]{:S(2)}, u32[]{:S(2)}) async-start(bf16[16,8,1024]{2,1,0:T(8,128)(2,1)} %fan_out.1), calls=%async_computation.3 | async-start | bytes 524288 | tf_op jit(solution)/shard_map/all_to_all | solution.py:337
  121.1 4.7 %collective-permute-start.7 = (f32[64,512]{1,0:T(8,128)S(1)}, f32[64,512]{1,0:T(8,128)S(1)}, u32[]{:S(2)}, u32[]{:S(2)}) collective-permute-start(f32[64,512]{1,0:T(8,128)S(1)} %fusion.8), channel_id=1, source_target_pairs={{0,128},{64,192},{128,0},{192,64},{256,384},{320,448},{384,256},{4... | collective-permute-start | bytes 393224 | tf_op jit(solution)/shard_map/ppermute | solution.py:319
  125.8 15.0 %collective-permute-done.7 = f32[64,512]{1,0:T(8,128)S(1)} collective-permute-done((f32[64,512]{1,0:T(8,128)S(1)}, f32[64,512]{1,0:T(8,128)S(1)}, u32[]{:S(2)}, u32[]{:S(2)}) %collective-permute-start.7) | collective-permute-done | bytes 131104 | tf_op jit(solution)/shard_map/ppermute | solution.py:319
  140.9 7.8 %collective-permute-start.8 = (bf16[64,256]{1,0:T(8,128)(2,1)S(1)}, bf16[64,256]{1,0:T(8,128)(2,1)S(1)}, u32[]{:S(2)}, u32[]{:S(2)}) collective-permute-start(bf16[64,256]{1,0:T(8,128)(2,1)S(1)} %select_convert_fusion), channel_id=1, source_target_pairs={{0,256},{64,320},{128,384},{192,448},{256,0},{320,64},{384,128},{4... | collective-permute-start | bytes 98312 | tf_op jit(solution)/shard_map/ppermute | solution.py:319
  149.0 2.0 %collective-permute-done.8 = bf16[64,256]{1,0:T(8,128)(2,1)S(1)} collective-permute-done((bf16[64,256]{1,0:T(8,128)(2,1)S(1)}, bf16[64,256]{1,0:T(8,128)(2,1)S(1)}, u32[]{:S(2)}, u32[]{:S(2)}) %collective-permute-start.8) | collective-permute-done | bytes 32800 | tf_op jit(solution)/shard_map/ppermute | solution.py:319
  (50 shorter events, 10.6 us)
Async XLA Ops:
  0.6 0.7 copy-start.5
  1.3 0.8 copy-start.3
  2.4 15.4 %collective-permute-start = (bf16[4,4096]{1,0:T(4,128)(2,1)S(1)}, bf16[4,4096]{1,0:T(4,128)(2,1)S(1)}, u32[]{:S(2)}, u32[]{:S(2)}) collective-permute-start(bf16[4,4096]{1,0:T(4,128)(2,1)S(1)} %get-tuple-element.19), channel_id=1, source_target_pairs={{0,258},{2,256},{64,322},{66,320},{128,386},{130,384},{192,450},{1... | collective-permute-start | bytes 98312 | tf_op jit(solution)/shard_map/ppermute | solution.py:268
  18.0 22.9 %copy-start = (bf16[1,8192,64]{1,2,0:T(8,128)(2,1)S(1)}, bf16[1,8192,64]{1,2,0:T(8,128)(2,1)}, u32[]{:S(2)}) copy-start(bf16[1,8192,64]{1,2,0:T(8,128)(2,1)} %param.15) | copy-start | bytes 3145732
  39.0 30.5 %collective-permute-start.1 = (bf16[128,4096]{1,0:T(8,128)(2,1)S(1)}, bf16[128,4096]{1,0:T(8,128)(2,1)}, u32[]{:S(2)}, u32[]{:S(2)}) collective-permute-start(bf16[128,4096]{1,0:T(8,128)(2,1)S(1)} %bitcast.27), channel_id=1, source_target_pairs={{0,1},{1,0},{2,3},{3,2},{4,5},{5,4},{6,7},{7,6},{8,9},{9,8},{10,11... | collective-permute-start | bytes 3145736 | tf_op jit(solution)/shard_map/ppermute | solution.py:273
  42.0 5.7 %copy-start.8 = (f32[1,4096]{1,0:T(1,128)S(1)}, f32[1,4096]{1,0:T(1,128)}, u32[]{:S(2)}) copy-start(f32[1,4096]{1,0:T(1,128)} %param.11) | copy-start | bytes 49156
  42.0 23.3 %copy-start.1 = (bf16[1,4096,128]{2,1,0:T(8,128)(2,1)S(1)}, bf16[1,4096,128]{2,1,0:T(8,128)(2,1)}, u32[]{:S(2)}) copy-start(bf16[1,4096,128]{2,1,0:T(8,128)(2,1)} %param.13) | copy-start | bytes 3145732
  42.0 40.2 %all-to-all-start.1 = ((bf16[16,64,512]{2,1,0:T(8,128)(2,1)}), bf16[16,64,512]{2,1,0:T(8,128)(2,1)S(1)}, u32[]{:S(2)}, u32[]{:S(2)}) async-start(bf16[16,64,512]{2,1,0:T(8,128)(2,1)} %split_columns.1), calls=%async_computation.1 | async-start | bytes 2097152 | tf_op jit(solution)/shard_map/all_to_all | solution.py:285
  47.8 5.6 %collective-permute-start.2 = (f32[1,4096]{1,0:T(1,128)S(1)}, f32[1,4096]{1,0:T(1,128)S(1)}, u32[]{:S(2)}, u32[]{:S(2)}) collective-permute-start(f32[1,4096]{1,0:T(1,128)S(1)} %copy-done.8), channel_id=1, source_target_pairs={{0,64},{64,0},{128,192},{192,128},{256,320},{320,256},{384,448},{4... | collective-permute-start | bytes 49160 | tf_op jit(solution)/shard_map/ppermute | solution.py:277
  53.4 6.5 %collective-permute-start.3 = (f32[1,4096]{1,0:T(1,128)S(1)}, f32[1,4096]{1,0:T(1,128)S(1)}, u32[]{:S(2)}, u32[]{:S(2)}) collective-permute-start(f32[1,4096]{1,0:T(1,128)S(1)} %add.33), channel_id=1, source_target_pairs={{0,128},{64,192},{128,0},{192,64},{256,384},{320,448},{384,256},{4... | collective-permute-start | bytes 49160 | tf_op jit(solution)/shard_map/ppermute | solution.py:277
  60.0 9.5 %collective-permute-start.4 = (f32[1,4096]{1,0:T(1,128)S(1)}, f32[1,4096]{1,0:T(1,128)S(1)}, u32[]{:S(2)}, u32[]{:S(2)}) collective-permute-start(f32[1,4096]{1,0:T(1,128)S(1)} %add.34), channel_id=1, source_target_pairs={{0,256},{64,320},{128,384},{192,448},{256,0},{320,64},{384,128},{4... | collective-permute-start | bytes 49160 | tf_op jit(solution)/shard_map/ppermute | solution.py:277
  65.3 1.2 copy-start.2
  71.8 16.3 %collective-permute-start.5 = (bf16[256,128]{1,0:T(8,128)(2,1)S(1)}, bf16[256,128]{1,0:T(8,128)(2,1)S(1)}, u32[]{:S(2)}, u32[]{:S(2)}) collective-permute-start(bf16[256,128]{1,0:T(8,128)(2,1)S(1)} %bitcast.33), channel_id=1, source_target_pairs={{0,2},{2,0},{1,3},{3,1},{4,6},{6,4},{5,7},{7,5},{8,10},{10,8},{9,1... | collective-permute-start | bytes 196616 | tf_op jit(solution)/shard_map/ppermute | solution.py:292
  91.5 7.3 %copy-start.7 = (bf16[1,64,2048]{2,1,0:T(8,128)(2,1)S(1)}, bf16[1,64,2048]{2,1,0:T(8,128)(2,1)}, u32[]{:S(2)}) copy-start(bf16[1,64,2048]{2,1,0:T(8,128)(2,1)} %param.12) | copy-start | bytes 786436
  91.5 17.1 %all-to-all-start.2 = ((bf16[16,16,1024]{2,1,0:T(8,128)(2,1)}), bf16[16,16,1024]{2,1,0:T(8,128)(2,1)S(1)}, u32[]{:S(2)}, u32[]{:S(2)}) async-start(bf16[16,16,1024]{2,1,0:T(8,128)(2,1)} %bitcast.13), calls=%async_computation.2 | async-start | bytes 1048576 | tf_op jit(solution)/shard_map/all_to_all | solution.py:330
  98.9 6.9 %collective-permute-start.6 = (bf16[64,1024]{1,0:T(8,128)(2,1)S(1)}, bf16[64,1024]{1,0:T(8,128)(2,1)S(1)}, u32[]{:S(2)}, u32[]{:S(2)}) collective-permute-start(bf16[64,1024]{1,0:T(8,128)(2,1)S(1)} %broadcast_select_fusion), channel_id=1, source_target_pairs={{0,64},{64,0},{128,192},{192,128},{256,320},{320,256},{384,448},{4... | collective-permute-start | bytes 393224 | tf_op jit(solution)/shard_map/ppermute | solution.py:319
  111.2 40.4 %all-to-all-start.3 = ((bf16[16,8,1024]{2,1,0:T(8,128)(2,1)}), bf16[16,8,1024]{2,1,0:T(8,128)(2,1)S(1)}, u32[]{:S(2)}, u32[]{:S(2)}) async-start(bf16[16,8,1024]{2,1,0:T(8,128)(2,1)} %fan_out.1), calls=%async_computation.3 | async-start | bytes 524288 | tf_op jit(solution)/shard_map/all_to_all | solution.py:337
  121.1 19.8 %collective-permute-start.7 = (f32[64,512]{1,0:T(8,128)S(1)}, f32[64,512]{1,0:T(8,128)S(1)}, u32[]{:S(2)}, u32[]{:S(2)}) collective-permute-start(f32[64,512]{1,0:T(8,128)S(1)} %fusion.8), channel_id=1, source_target_pairs={{0,128},{64,192},{128,0},{192,64},{256,384},{320,448},{384,256},{4... | collective-permute-start | bytes 393224 | tf_op jit(solution)/shard_map/ppermute | solution.py:319
  140.9 7.8 %copy-start.4 = (bf16[8,4096]{1,0:T(8,128)(2,1)S(1)}, bf16[8,4096]{1,0:T(8,128)(2,1)}, u32[]{:S(2)}) copy-start(bf16[8,4096]{1,0:T(8,128)(2,1)} %tokens.2) | copy-start | bytes 196612
  140.9 7.8 %copy-start.6 = (f32[8,2]{0,1:T(2,128)S(1)}, f32[8,2]{0,1:T(2,128)}, u32[]{:S(2)}) copy-start(f32[8,2]{0,1:T(2,128)} %param.10) | copy-start | bytes 196
  140.9 10.1 %collective-permute-start.8 = (bf16[64,256]{1,0:T(8,128)(2,1)S(1)}, bf16[64,256]{1,0:T(8,128)(2,1)S(1)}, u32[]{:S(2)}, u32[]{:S(2)}) collective-permute-start(bf16[64,256]{1,0:T(8,128)(2,1)S(1)} %select_convert_fusion), channel_id=1, source_target_pairs={{0,256},{64,320},{128,384},{192,448},{256,0},{320,64},{384,128},{4... | collective-permute-start | bytes 98312 | tf_op jit(solution)/shard_map/ppermute | solution.py:319
